TPU v7x, 128 devices: a whole 4x4x4 slice. The times are simulated.
128 devices in a mesh: row: 4 (over x), col: 32 (over y, z, core).
Axes of the slice: x: 4, y: 4, z: 4, core: 2. Of those that a mesh axis runs over, the one named last changes fastest.
Arguments:
- ancestor_inverse: float32 [16384, 16384], P('col', 'row'), as said below
- panels: float32 [2, 16384, 512], P(None, ('col', 'row')), may hold values from -0.1875 to 0.1875
- pattern: int32 [2, 128, 2], replicated, may hold values 0 or 1
- diag_inverse: float32 [2, 512, 512], replicated, may hold values from -6 to 6
- link_panel: float32 [512, 512], replicated, may hold values from -0.25 to 0.25
- block_list: int32 [32, 4, 32], P('col', 'row'), may hold values from 0 to 7
- gauge_owner: int32 [32, 4, 32], P('col', 'row'), may hold values from 0 to 31, each once within a row
- gauge_weight: float32 [4, 32, 512], P('row', 'col'), may hold values from -0.25 to 0.25
Outputs:
- y_first: float32 [16384, 512], P(('col', 'row'))
- diag_first: float32 [512, 512], replicated
- y_second: float32 [16384, 512], P(('col', 'row'))
- cross_second: float32 [512, 512], replicated
- diag_second: float32 [512, 512], replicated
- gauge_response: float32 [4, 32, 512], P('row', 'col')
Inputs may be any that keep to these rules, and one draw needn't show every extreme that they name: `ancestor_inverse`: with its columns put in natural order the matrix is symmetric.
All inputs are finite; a program needn't handle non-finite values.
Results may differ from a plain program's by a relative error of at most 0.000092.
Values sent between devices are 32-bit elements; how exact they have to be, the bound alone decides.
No kernel may reach another device: no remote copies, remote signals or barrier semaphores. Data moves between devices by JAX's collectives and lax.ppermute only.
A program may use at most 128 MiB of HBM per device.

v0:
```python
import jax
import jax.numpy as jnp
from jax import lax
from jax.sharding import PartitionSpec as P

NIB = 8


HIGHEST_PRECISION = lax.Precision.HIGHEST


def matmul(left, right):
    return jnp.dot(left, right, precision=HIGHEST_PRECISION, preferred_element_type=jnp.float32)


def inner_product(left, right):
    return lax.dot_general(
        left,
        right,
        (((0,), (0,)), ((), ())),
        precision=HIGHEST_PRECISION,
        preferred_element_type=jnp.float32,
    )


def apply_pattern(panel, pattern_step, seg_index):
    tile_flags = lax.dynamic_index_in_dim(pattern_step, seg_index, 0, keepdims=False).astype(
        jnp.float32
    )
    seg_rows, panel_width = panel.shape
    tile_count = tile_flags.shape[0]
    shaped = (
        panel.reshape(seg_rows, tile_count, panel_width // tile_count) * tile_flags[None, :, None]
    )
    return shaped.reshape(seg_rows, panel_width)


def inverse_slab(ancestor, panel_seg):
    partial_rows = matmul(ancestor, lax.all_gather(panel_seg, "col", axis=0, tiled=True))
    return lax.psum_scatter(partial_rows, "row", scatter_dimension=0, tiled=True)


def local(
    ancestor_inverse,
    panels,
    pattern,
    diag_inverse,
    link_panel,
    block_list,
    gauge_owner,
    gauge_weight,
):
    grid_rows = lax.axis_size("row")
    grid_cols = lax.axis_size("col")
    seg_index = lax.axis_index("col") * grid_rows + lax.axis_index("row")
    first_panel = apply_pattern(panels[0], pattern[0], seg_index)
    second_panel = apply_pattern(panels[1], pattern[1], seg_index)
    y_first = -inverse_slab(ancestor_inverse, first_panel)
    first_terms = lax.psum(inner_product(first_panel, y_first), ("row", "col"))
    diag_first = diag_inverse[0] - first_terms
    cross_terms = lax.psum(inner_product(y_first, second_panel), ("row", "col"))
    y_second = -(inverse_slab(ancestor_inverse, second_panel) + matmul(y_first, link_panel))
    second_terms = lax.psum(inner_product(second_panel, y_second), ("row", "col"))
    cross_second = -(cross_terms + matmul(diag_first, link_panel))
    diag_second = diag_inverse[1] - second_terms - inner_product(link_panel, cross_second)
    seg_rows, panel_width = y_second.shape
    block_rows = seg_rows // NIB
    blocks = y_second.reshape(NIB, block_rows * panel_width)
    owners = gauge_owner[0, 0]
    picks = block_list[0, 0]
    owner_match = (owners[None, :] == jnp.arange(grid_cols, dtype=jnp.int32)[:, None]).astype(
        jnp.float32
    )
    block_match = (picks[:, None] == jnp.arange(NIB, dtype=jnp.int32)[None, :]).astype(jnp.float32)
    selector = matmul(owner_match, block_match)
    outgoing = matmul(selector, blocks)
    received = lax.all_to_all(outgoing, "col", split_axis=0, concat_axis=0, tiled=True)
    received_rows = received.reshape(grid_cols * block_rows, panel_width)
    weights = gauge_weight[0, 0]
    gauge_response = matmul(weights[None, :], received_rows).reshape(1, 1, panel_width)
    return (y_first, diag_first, y_second, cross_second, diag_second, gauge_response)


def solution(mesh):
    in_specs = (
        P("col", "row"),
        P(None, ("col", "row"), None),
        P(),
        P(),
        P(),
        P("col", "row", None),
        P("col", "row", None),
        P("row", "col", None),
    )
    out_specs = (
        P(("col", "row"), None),
        P(),
        P(("col", "row"), None),
        P(),
        P(),
        P("row", "col", None),
    )
    return jax.shard_map(local, mesh=mesh, in_specs=in_specs, out_specs=out_specs, check_vma=False)
```

profile of v0, /device:TPU:1, one launch (start us, length us, event | category | flops | bytes accessed | tf_op | source)
XLA Modules:
  0.0 363.5 jit_solution(13496992720899328515)
XLA Ops:
  7.2 0.8 fusion.12
  8.4 1.9 bitcast_multiply_fusion
  10.3 0.7 all-gather.5.cloned.1.call-update
  11.1 56.5 %all-gather.3.cloned.1.call-done = f32[4096,512]{1,0:T(8,128)} async-done(((f32[128,512]{1,0:T(8,128)}), f32[4096,512]{1,0:T(8,128)}) %all-gather.3.cloned.1.call-update) | async-done | bytes 8388624 | tf_op jit(solution)/shard_map/all_gather | solution.py:39
  67.5 30.1 %convolution_bitcast_fusion.3 = f32[512,512]{0,1:T(8,128)} fusion(f32[4096,512]{1,0:T(8,128)} %all-gather.3.cloned.1.call-done, f32[512,4096]{1,0:T(8,128)} %param.8), kind=kOutput, calls=%fused_computation.6 | convolution fusion | flops 12884901888 | bytes 17825792 | tf_op jit(solution)/shard_map/dot_general | solution.py:13
  97.9 25.0 %all-gather.5.cloned.1.call-done = f32[4096,512]{1,0:T(8,128)} async-done(((f32[128,512]{1,0:T(8,128)}), f32[4096,512]{1,0:T(8,128)}) %all-gather.5.cloned.1.call-update) | async-done | bytes 8388624 | tf_op jit(solution)/shard_map/all_gather | solution.py:39
  122.9 30.1 %convolution_bitcast_fusion.2 = f32[512,512]{0,1:T(8,128)} fusion(f32[4096,512]{1,0:T(8,128)} %all-gather.5.cloned.1.call-done, f32[512,4096]{1,0:T(8,128)} %param.8), kind=kOutput, calls=%fused_computation.5 | convolution fusion | flops 12884901888 | bytes 17825792 | tf_op jit(solution)/shard_map/dot_general | solution.py:13
  153.0 0.3 all-reduce.3.cloned.1.call-start
  153.3 21.1 %reduce-scatter.5.cloned.1.call-done = f32[128,512]{0,1:T(8,128)} async-done(((f32[512,512]{0,1:T(8,128)}), f32[128,512]{0,1:T(8,128)}) %reduce-scatter.5.cloned.1.call-update) | async-done | bytes 262160 | tf_op jit(solution)/shard_map/reduce_scatter | solution.py:40
  174.4 2.8 fusion.2
  177.3 2.0 fusion.13
  179.3 2.9 fusion.7
  182.2 3.0 fusion.10
  185.6 1.0 convolution_bitcast_fusion
  186.7 2.1 copy.26
  188.7 9.0 %all-to-all-start = ((f32[32,1,8192]{2,1,0:T(1,128)}), f32[32,1,8192]{2,1,0:T(1,128)S(1)}, u32[]{:S(2)}, u32[]{:S(2)}) async-start(f32[32,1,8192]{2,1,0:T(1,128)} %copy.26), calls=%async_computation.2 | async-start | bytes 2097152 | tf_op jit(solution)/shard_map/all_to_all | solution.py:77
  197.8 0.8 copy.27
  198.6 17.2 %all-to-all-done = f32[32,1,8192]{2,1,0:T(1,128)S(1)} async-done(((f32[32,1,8192]{2,1,0:T(1,128)}), f32[32,1,8192]{2,1,0:T(1,128)S(1)}, u32[]{:S(2)}, u32[]{:S(2)}) %all-to-all-start) | async-done | bytes 1048608 | tf_op jit(solution)/shard_map/all_to_all | solution.py:77
  215.9 2.6 reduce.2
  218.7 1.2 convolution_bitcast_fusion.4
  219.9 127.0 %all-reduce.3.cloned.1.call-done = (f32[512,512]{1,0:T(8,128)}, f32[512,512]{1,0:T(8,128)}, f32[512,512]{1,0:T(8,128)}) async-done(((f32[512,512]{1,0:T(8,128)}, f32[512,512]{1,0:T(8,128)}, f32[512,512]{1,0:T(8,128)}), (f32[512,512]{1,0:T(8,128)}, f32[512,512]{1,0:T(8,128)}, f32[512,512]{1,0:T(8,128)})) %all-reduce.3.cloned.1.call-update) | async-done | bytes 3145744 | tf_op jit(solution)/shard_map/psum | solution.py:59
  346.9 1.7 bitcast_subtract_fusion.1
  348.6 3.5 fusion.1
  352.2 4.8 %fusion = f32[512,512]{1,0:T(8,128)} fusion(f32[512,512]{1,0:T(8,128)S(1)} %fusion.1, f32[512,512]{1,0:T(8,128)S(1)} %copy-done, f32[512,512]{1,0:T(8,128)} %get-tuple-element.26, f32[2,512,512]{2,1,0:T(8,128)} %param.11), kind=kOutput, calls=%fused_computation.2 | convolution fusion | flops 1611137024 | bytes 5242880 | tf_op jit(solution)/shard_map/dot_general | solution.py:17
  (39 shorter events, 1.5 us)
Async XLA Ops:
  7.2 167.3 %copy-start = (f32[512,512]{1,0:T(8,128)S(1)}, f32[512,512]{1,0:T(8,128)}, u32[]{:S(2)}) copy-start(f32[512,512]{1,0:T(8,128)} %param.12) | copy-start | bytes 3145732
  7.2 60.4 %all-gather.3.cloned.1.call-start = ((), (), s32[]{:S(2)}) async-start(), calls=%async_computation.3 | async-start | bytes 8650752 | tf_op jit(solution)/shard_map/all_gather | solution.py:39
  10.3 112.6 %all-gather.5.cloned.1.call-start = ((), (), s32[]{:S(2)}) async-start(), calls=%async_computation.5 | async-start | bytes 8650752 | tf_op jit(solution)/shard_map/all_gather | solution.py:39
  11.0 142.3 %reduce-scatter.3.cloned.1.call-start = ((), (), s32[]{:S(2)}) async-start(), calls=%async_computation.4 | async-start | bytes 1310720 | tf_op jit(solution)/shard_map/reduce_scatter | solution.py:40
  97.6 79.6 %copy-start.4 = (f32[128,512]{1,0:T(8,128)S(1)}, f32[128,512]{1,0:T(8,128)}, u32[]{:S(2)}) copy-start(f32[128,512]{1,0:T(8,128)} %get-tuple-element.27) | copy-start | bytes 786436
  97.6 84.5 %copy-start.5 = (f32[128,512]{1,0:T(8,128)S(1)}, f32[128,512]{1,0:T(8,128)}, u32[]{:S(2)}) copy-start(f32[128,512]{1,0:T(8,128)} %get-tuple-element.28) | copy-start | bytes 786436
  97.7 76.8 %reduce-scatter.5.cloned.1.call-start = ((), (), s32[]{:S(2)}) async-start(), calls=%async_computation.6 | async-start | bytes 1310720 | tf_op jit(solution)/shard_map/reduce_scatter | solution.py:40
  153.0 32.2 %copy-start.8 = (s32[1,1,32]{2,1,0:T(1,128)S(1)}, s32[1,1,32]{2,1,0:T(1,128)}, u32[]{:S(2)}) copy-start(s32[1,1,32]{2,1,0:T(1,128)} %param.13) | copy-start | bytes 388
  153.0 32.2 %copy-start.9 = (s32[1,1,32]{2,1,0:T(1,128)S(1)}, s32[1,1,32]{2,1,0:T(1,128)}, u32[]{:S(2)}) copy-start(s32[1,1,32]{2,1,0:T(1,128)} %param.14) | copy-start | bytes 388
  153.0 193.8 %all-reduce.3.cloned.1.call-start = ((), (), s32[]{:S(2)}) async-start(), calls=%async_computation.7 | async-start | bytes 6291456 | tf_op jit(solution)/shard_map/psum | solution.py:59
  153.3 44.4 %copy-start.3 = (f32[128,512]{0,1:T(8,128)S(1)}, f32[128,512]{0,1:T(8,128)}, u32[]{:S(2)}) copy-start(f32[128,512]{0,1:T(8,128)} %reduce-scatter.3.cloned.1.call-done) | copy-start | bytes 786436
  182.2 36.5 %copy-start.7 = (f32[1,1,512]{2,1,0:T(1,128)S(1)}, f32[1,1,512]{2,1,0:T(1,128)}, u32[]{:S(2)}) copy-start(f32[1,1,512]{2,1,0:T(1,128)} %param.15) | copy-start | bytes 6148
  185.6 3.2 copy-start.6
  188.7 27.2 %all-to-all-start = ((f32[32,1,8192]{2,1,0:T(1,128)}), f32[32,1,8192]{2,1,0:T(1,128)S(1)}, u32[]{:S(2)}, u32[]{:S(2)}) async-start(f32[32,1,8192]{2,1,0:T(1,128)} %copy.26), calls=%async_computation.2 | async-start | bytes 2097152 | tf_op jit(solution)/shard_map/all_to_all | solution.py:77
  348.6 8.3 %copy-start.1 = (f32[512,512]{1,0:T(8,128)}, f32[512,512]{1,0:T(8,128)S(1)}, u32[]{:S(2)}) copy-start(f32[512,512]{1,0:T(8,128)S(1)} %bitcast_subtract_fusion.1) | copy-start | bytes 3145732
  352.2 4.8 %copy-start.2 = (f32[512,512]{1,0:T(8,128)}, f32[512,512]{1,0:T(8,128)S(1)}, u32[]{:S(2)}) copy-start(f32[512,512]{1,0:T(8,128)S(1)} %fusion.1) | copy-start | bytes 3145732
Sparse Core Ops, SparseCore 0:
  10.9 56.6 all-gather.2
  70.4 52.5 all-gather.4
  125.9 21.1 reduce-scatter.2
  153.2 21.2 reduce-scatter.4
  185.3 161.5 all-reduce.2
where the time goes:
time: 364 us; the launch traced here: 363 us
  waiting for transfers between devices  248 us (68%)
  matrix products  81.6 us (22%)
  between operations  14 us (4%)
  starting transfers between devices  9.63 us (3%)
  other arithmetic  6.45 us (2%)
  local copies, waits for them, and re-layouts  4.26 us (1%)
    psum x1, waiting for transfers between devices, local(): first_terms = lax.psum(inner_product(first_panel, y_first), ('row', 'col'))  127 us
    all_gather x2, waiting for transfers between devices, inverse_slab(): lax.all_gather(panel_seg, 'col', axis=0, tiled=True)  81.5 us
    dot_general x7, matrix products, matmul(): jnp.dot(left, right, precision=HIGHEST_PRECISION, preferred_element_type=...  69 us
    reduce_scatter x2, waiting for transfers between devices, inverse_slab(): lax.psum_scatter(partial_rows, 'row', scatter_dimension=0, tiled=True)  21.1 us
    all_to_all x1, waiting for transfers between devices, local(): lax.all_to_all(outgoing, 'col', split_axis=0, concat_axis=0, tiled=True)  17.2 us
    dot_general x4, matrix products, inner_product(): lax.dot_general(left, right, (((0,), (0,)), ((), ())), precision=HIGHEST_...  12.6 us
    all_to_all x1, starting transfers between devices, local(): lax.all_to_all(outgoing, 'col', split_axis=0, concat_axis=0, tiled=True)  9.03 us
  transfers between devices with their start and end apart: 6, of which 5 were waited for; matrix products, arithmetic and copies ran while one was open for 19% of the time, Pallas kernels for 0%

commit v1 on v0

v1 whole, which is shorter than its diff:
```python
import jax
import jax.numpy as jnp
from jax import lax
from jax.sharding import Mesh, PartitionSpec as P

NIB = 8
IBR = 16
HIGH = lax.Precision.HIGH
COL = ("y", "z", "core")
CHIPS = ("x", "y", "z")


def dot(left, right, left_dim=1, right_dim=0, precision=HIGH):
    return lax.dot_general(
        left,
        right,
        (((left_dim,), (right_dim,)), ((), ())),
        precision=precision,
        preferred_element_type=jnp.float32,
    )


def swap_core(value):
    return lax.ppermute(value, "core", [(0, 1), (1, 0)])


def spread(value, axes, count):
    copies = jnp.broadcast_to(value[None], (count,) + value.shape)
    return lax.all_to_all(copies, axes, 0, 0, tiled=True)


def all_sum(partial):
    rows, width = partial.shape
    core = lax.axis_index("core")
    halves = partial.reshape(2, rows // 2, width)
    mine = lax.dynamic_index_in_dim(halves, core, 0, keepdims=False)
    theirs = lax.dynamic_index_in_dim(halves, 1 - core, 0, keepdims=False)
    half = mine + swap_core(theirs)
    pieces = half.reshape(64, rows // 128, width)
    part = lax.all_to_all(pieces, CHIPS, 0, 0, tiled=True).sum(0)
    whole = spread(part, CHIPS, 64).reshape(rows // 2, width)
    other = swap_core(whole)
    first = core == 0
    return jnp.concatenate([jnp.where(first, whole, other), jnp.where(first, other, whole)], 0)


def local(
    ancestor,
    panels,
    pattern,
    diag_inverse,
    link,
    block_list,
    gauge_owner,
    gauge_weight,
):
    row = lax.axis_index("x")
    col = lax.axis_index("y") * 8 + lax.axis_index("z") * 2 + lax.axis_index("core")
    flags = lax.dynamic_index_in_dim(pattern, col * 4 + row, 1, keepdims=False)
    flags = jnp.repeat(flags.astype(jnp.float32), 256, axis=1)
    masked = panels * flags[:, None, :]
    both = jnp.concatenate([masked[0], masked[1]], axis=1)
    gathered = lax.all_gather(both, COL, axis=0, tiled=True)
    own_rows = spread(both, "x", 4).reshape(512, 1024)
    weights = lax.all_to_all(gauge_weight.reshape(32, IBR), COL, 0, 0, tiled=True)
    owner_match = (
        gauge_owner[0, 0][None, :] == jnp.arange(32, dtype=jnp.int32)[:, None]
    ).astype(jnp.float32)
    block_match = (
        block_list[0, 0][:, None] == jnp.arange(NIB, dtype=jnp.int32)[None, :]
    ).astype(jnp.float32)
    selector = dot(owner_match, block_match, precision=lax.Precision.HIGHEST)
    combine = (selector[:, :, None] * weights[:, None, :]).reshape(32, NIB * IBR)

    z = dot(ancestor, gathered)
    g_first = dot(own_rows[:, :512], z[:, :512], 0, 0)
    g_cross = dot(z[:, :512], own_rows[:, 512:], 0, 0)
    g_second = dot(own_rows[:, 512:], z[:, 512:], 0, 0)
    z_rows = lax.all_to_all(z.reshape(4, 128, 1024), "x", 0, 0, tiled=True).sum(0)
    grams = all_sum(jnp.concatenate([g_first, g_cross, g_second], 0))
    y_first = -z_rows[:, :512]
    y_second = -(z_rows[:, 512:] + dot(y_first, link))
    shares = dot(combine, y_second)
    gauge = lax.all_to_all(shares, COL, 0, 0, tiled=True).sum(0).reshape(1, 1, 512)
    diag_first = diag_inverse[0] + grams[:512]
    cross = grams[512:1024]
    cross_second = cross - dot(diag_first, link)
    diag_second = (
        diag_inverse[1] + grams[1024:] - dot(cross, link, 0, 0) - dot(link, cross_second, 0, 0)
    )
    return (y_first, diag_first, y_second, cross_second, diag_second, gauge)


def solution(mesh):
    grid = Mesh(mesh.devices.reshape(4, 4, 4, 2), ("x", "y", "z", "core"))
    in_specs = (
        P(COL, "x"),
        P(None, COL + ("x",), None),
        P(),
        P(),
        P(),
        P(COL, "x", None),
        P(COL, "x", None),
        P("x", COL, None),
    )
    out_specs = (
        P(COL + ("x",), None),
        P(),
        P(COL + ("x",), None),
        P(),
        P(),
        P("x", COL, None),
    )
    return jax.shard_map(local, mesh=grid, in_specs=in_specs, out_specs=out_specs, check_vma=False)
```

time: 364 us -> 267 us (0.73)
  waiting for transfers between devices: 248 us -> 132 us
  matrix products: 81.6 us -> 31.3 us
  blocking collectives: 0 us -> 32.3 us
  starting transfers between devices: 9.63 us -> 35.1 us
  local copies, waits for them, and re-layouts: 4.26 us -> 10.4 us
  other arithmetic: 6.45 us -> 10.8 us
    psum x1 -> x0, waiting for transfers between devices: 127 us -> none  [local(): first_terms = lax.psum(inner_product(first_panel, y_first), ('row', 'col'))]
    dot_general x11 -> x10, matrix products: 81.6 us -> 31.3 us  [dot(): lax.dot_general(left, right, (((left_dim,), (right_dim,)), ((), ())), pre...]
    all_to_all x1 -> x5, waiting for transfers between devices: 17.2 us -> 58.9 us  [the longest x1 25.8 us: all_sum(): part = lax.all_to_all(pieces, CHIPS, 0, 0, tiled=True).sum(0)]
    all_to_all x0 -> x1, blocking collectives: none -> 32.3 us  [spread(): return lax.all_to_all(copies, axes, 0, 0, tiled=True)]
    all_to_all x1 -> x5, starting transfers between devices: 9.03 us -> 31.7 us  [the longest x1 8.28 us: all_sum(): part = lax.all_to_all(pieces, CHIPS, 0, 0, tiled=True).sum(0)]
    reduce_scatter x2 -> x0, waiting for transfers between devices: 21.1 us -> none  [inverse_slab(): lax.psum_scatter(partial_rows, 'row', scatter_dimension=0, tiled=True)]
    all_gather x2 -> x1, waiting for transfers between devices: 81.5 us -> 69.4 us  [local(): gathered = lax.all_gather(both, COL, axis=0, tiled=True)]
  transfers between devices with their start and end apart: 6 -> 8, of which waited for: 5 -> 6; matrix products, arithmetic and copies ran while one was open for 19% -> 11% of each run, Pallas kernels for 0% -> 0%
where the time goes in v1:
time: 267 us; the launch traced here: 266 us
  waiting for transfers between devices  132 us (49%)
  starting transfers between devices  35.1 us (13%)
  blocking collectives  32.3 us (12%)
  matrix products  31.3 us (12%)
  between operations  14.3 us (5%)
  other arithmetic  10.8 us (4%)
  local copies, waits for them, and re-layouts  10.4 us (4%)
    all_gather x1, waiting for transfers between devices, local(): gathered = lax.all_gather(both, COL, axis=0, tiled=True)  69.4 us
    all_to_all x1, blocking collectives, spread(): return lax.all_to_all(copies, axes, 0, 0, tiled=True)  32.3 us
    dot_general x10, matrix products, dot(): lax.dot_general(left, right, (((left_dim,), (right_dim,)), ((), ())), pre...  31.3 us
    all_to_all x1, waiting for transfers between devices, all_sum(): part = lax.all_to_all(pieces, CHIPS, 0, 0, tiled=True).sum(0)  25.8 us
    all_to_all x1, waiting for transfers between devices, local(): lax.all_to_all(z.reshape(4, 128, 1024), 'x', 0, 0, tiled=True).sum(0)  19 us
    all_to_all x1, starting transfers between devices, all_sum(): part = lax.all_to_all(pieces, CHIPS, 0, 0, tiled=True).sum(0)  8.28 us
    all_to_all x1, starting transfers between devices, local(): lax.all_to_all(shares, COL, 0, 0, tiled=True).sum(0).reshape(1, 1, 512)  7.64 us
    all_to_all x1, waiting for transfers between devices, local(): lax.all_to_all(shares, COL, 0, 0, tiled=True).sum(0).reshape(1, 1, 512)  7.36 us
  transfers between devices with their start and end apart: 8, of which 6 were waited for; matrix products, arithmetic and copies ran while one was open for 11% of the time, Pallas kernels for 0%

profile of v1, /device:TPU:1, one launch (start us, length us, event | category | flops | bytes accessed | tf_op | source)
XLA Modules:
  0.0 265.8 jit_solution(2948248204228471022)
XLA Ops:
  10.2 2.6 broadcast_in_dim.7
  12.9 4.8 %all-to-all-start.1 = ((f32[4,128,1024]{2,1,0:T(8,128)}), f32[4,128,1024]{2,1,0:T(8,128)S(1)}, u32[]{:S(2)}, u32[]{:S(2)}) async-start(f32[4,128,1024]{2,1,0:T(8,128)} %broadcast_in_dim.7), calls=%async_computation.1 | async-start | bytes 4194304 | tf_op jit(solution)/shard_map/all_to_all | solution.py:29
  17.7 69.4 %all-gather.2.cloned.1.call-done = f32[4096,1024]{1,0:T(8,128)} async-done(((f32[128,1024]{1,0:T(8,128)}), f32[4096,1024]{1,0:T(8,128)}) %all-gather.2.cloned.1.call-update) | async-done | bytes 16777232 | tf_op jit(solution)/shard_map/all_gather | solution.py:63
  87.1 19.4 %fusion.16 = f32[1024,512]{0,1:T(8,128)} fusion(f32[4096,1024]{1,0:T(8,128)} %all-gather.2.cloned.1.call-done, f32[512,4096]{1,0:T(8,128)} %param.8), kind=kOutput, calls=%fused_computation.38 | convolution fusion | flops 12884901888 | bytes 27262976 | tf_op jit(solution)/shard_map/dot_general | solution.py:14
  106.5 2.3 fusion.3
  108.8 2.3 fusion.8
  111.1 2.3 fusion.5
  113.6 1.6 copy-done.1
  115.9 3.3 %collective-permute-done = f32[768,512]{1,0:T(8,128)} collective-permute-done((f32[768,512]{1,0:T(8,128)S(1)}, f32[768,512]{1,0:T(8,128)}, u32[]{:S(2)}, u32[]{:S(2)}) %collective-permute-start) | collective-permute-done | bytes 1572896 | tf_op jit(solution)/shard_map/ppermute | solution.py:24
  119.2 2.2 bitcast_add_fusion
  121.4 1.5 reshape.52
  122.9 8.3 %all-to-all-start.2 = ((f32[64,12,512]{2,1,0:T(8,128)}), f32[64,12,512]{2,1,0:T(8,128)S(1)}, u32[]{:S(2)}, u32[]{:S(2)}) async-start(f32[64,12,512]{2,1,0:T(8,128)} %reshape.52), calls=%async_computation.2 | async-start | bytes 4194304 | tf_op jit(solution)/shard_map/all_to_all | solution.py:40
  133.1 25.8 %all-to-all-done.2 = f32[64,12,512]{2,1,0:T(8,128)S(1)} async-done(((f32[64,12,512]{2,1,0:T(8,128)}), f32[64,12,512]{2,1,0:T(8,128)S(1)}, u32[]{:S(2)}, u32[]{:S(2)}) %all-to-all-start.2) | async-done | bytes 1572896 | tf_op jit(solution)/shard_map/all_to_all | solution.py:40
  158.9 6.5 %all-to-all-start.4 = ((f32[32,1,16]{2,1,0:T(1,128)}), f32[32,1,16]{2,1,0:T(1,128)S(1)}, u32[]{:S(2)}, u32[]{:S(2)}) async-start(f32[32,1,16]{2,1,0:T(1,128)} %bitcast.13), calls=%async_computation.4 | async-start | bytes 32768 | tf_op jit(solution)/shard_map/all_to_all | solution.py:65
  165.5 6.8 %all-to-all-done.4 = f32[32,1,16]{2,1,0:T(1,128)S(1)} async-done(((f32[32,1,16]{2,1,0:T(1,128)}), f32[32,1,16]{2,1,0:T(1,128)S(1)}, u32[]{:S(2)}, u32[]{:S(2)}) %all-to-all-start.4) | async-done | bytes 2080 | tf_op jit(solution)/shard_map/all_to_all | solution.py:65
  172.6 32.3 %all_to_all.38 = f32[64,12,512]{2,1,0:T(8,128)S(1)} all-to-all(f32[64,12,512]{2,1,0:T(8,128)S(1)} %broadcast_in_dim.8), channel_id=1, replica_groups=mesh['x'=4,'y'=4,'z'=4,'core'=2] {'x','y','z'}, dimensions={0} | all-to-all | bytes 3145728 | tf_op jit(solution)/shard_map/all_to_all | solution.py:29
  204.9 4.4 %all-to-all-start = ((f32[4,128,1024]{2,1,0:T(8,128)}), f32[4,128,1024]{2,1,0:T(8,128)}, u32[]{:S(2)}, u32[]{:S(2)}) async-start(f32[4,128,1024]{2,1,0:T(8,128)} %bitcast.3), calls=%async_computation | async-start | bytes 4194304 | tf_op jit(solution)/shard_map/all_to_all | solution.py:79
  210.7 2.9 %collective-permute-start.1 = (f32[768,512]{1,0:T(8,128)}, f32[768,512]{1,0:T(8,128)}, u32[]{:S(2)}, u32[]{:S(2)}) collective-permute-start(f32[768,512]{1,0:T(8,128)} %reshape.53), channel_id=1, source_target_pairs={{0,1},{1,0},{2,3},{3,2},{4,5},{5,4},{6,7},{7,6},{8,9},{9,8},{10,11... | collective-permute-start | bytes 4718600 | tf_op jit(solution)/shard_map/ppermute | solution.py:24
  213.9 19.0 %all-to-all-done = f32[4,128,1024]{2,1,0:T(8,128)} async-done(((f32[4,128,1024]{2,1,0:T(8,128)}), f32[4,128,1024]{2,1,0:T(8,128)}, u32[]{:S(2)}, u32[]{:S(2)}) %all-to-all-start) | async-done | bytes 2097184 | tf_op jit(solution)/shard_map/all_to_all | solution.py:79
  232.9 1.8 reduce_sum.27
  236.8 7.6 %all-to-all-start.5 = ((f32[32,1,512]{2,1,0:T(1,128)}), f32[32,1,512]{2,1,0:T(1,128)S(1)}, u32[]{:S(2)}, u32[]{:S(2)}) async-start(f32[32,1,512]{2,1,0:T(1,128)} %copy.21), calls=%async_computation.5 | async-start | bytes 131072 | tf_op jit(solution)/shard_map/all_to_all | solution.py:84
  244.4 7.4 %all-to-all-done.5 = f32[32,1,512]{2,1,0:T(1,128)S(1)} async-done(((f32[32,1,512]{2,1,0:T(1,128)}), f32[32,1,512]{2,1,0:T(1,128)S(1)}, u32[]{:S(2)}, u32[]{:S(2)}) %all-to-all-start.5) | async-done | bytes 65568 | tf_op jit(solution)/shard_map/all_to_all | solution.py:84
  252.5 1.9 broadcast_select_fusion
  256.8 2.2 fusion.2
  (51 shorter events, 13.0 us)
Async XLA Ops:
  7.2 227.5 %copy-start = (f32[512,512]{1,0:T(8,128)S(1)}, f32[512,512]{1,0:T(8,128)}, u32[]{:S(2)}) copy-start(f32[512,512]{1,0:T(8,128)} %param.12) | copy-start | bytes 3145732
  7.2 79.9 %all-gather.2.cloned.1.call-start = ((), (), s32[]{:S(2)}) async-start(), calls=%async_computation.6 | async-start | bytes 17301504 | tf_op jit(solution)/shard_map/all_gather | solution.py:63
  12.9 93.7 %all-to-all-start.1 = ((f32[4,128,1024]{2,1,0:T(8,128)}), f32[4,128,1024]{2,1,0:T(8,128)S(1)}, u32[]{:S(2)}, u32[]{:S(2)}) async-start(f32[4,128,1024]{2,1,0:T(8,128)} %broadcast_in_dim.7), calls=%async_computation.1 | async-start | bytes 4194304 | tf_op jit(solution)/shard_map/all_to_all | solution.py:29
  113.6 1.6 copy-start.1
  115.4 3.8 %collective-permute-start = (f32[768,512]{1,0:T(8,128)S(1)}, f32[768,512]{1,0:T(8,128)}, u32[]{:S(2)}, u32[]{:S(2)}) collective-permute-start(f32[768,512]{1,0:T(8,128)S(1)} %dynamic-slice_bitcast_fusion), channel_id=1, source_target_pairs={{0,1},{1,0},{2,3},{3,2},{4,5},{5,4},{6,7},{7,6},{8,9},{9,8},{10,11... | collective-permute-start | bytes 4718600 | tf_op jit(solution)/shard_map/ppermute | solution.py:24
  122.9 8.8 %copy-start.8 = (f32[1,1,512]{2,1,0:T(1,128)S(1)}, f32[1,1,512]{2,1,0:T(1,128)}, u32[]{:S(2)}) copy-start(f32[1,1,512]{2,1,0:T(1,128)} %param.15) | copy-start | bytes 6148
  122.9 35.9 %all-to-all-start.2 = ((f32[64,12,512]{2,1,0:T(8,128)}), f32[64,12,512]{2,1,0:T(8,128)S(1)}, u32[]{:S(2)}, u32[]{:S(2)}) async-start(f32[64,12,512]{2,1,0:T(8,128)} %reshape.52), calls=%async_computation.2 | async-start | bytes 4194304 | tf_op jit(solution)/shard_map/all_to_all | solution.py:40
  158.9 13.4 %all-to-all-start.4 = ((f32[32,1,16]{2,1,0:T(1,128)}), f32[32,1,16]{2,1,0:T(1,128)S(1)}, u32[]{:S(2)}, u32[]{:S(2)}) async-start(f32[32,1,16]{2,1,0:T(1,128)} %bitcast.13), calls=%async_computation.4 | async-start | bytes 32768 | tf_op jit(solution)/shard_map/all_to_all | solution.py:65
  204.9 28.0 %all-to-all-start = ((f32[4,128,1024]{2,1,0:T(8,128)}), f32[4,128,1024]{2,1,0:T(8,128)}, u32[]{:S(2)}, u32[]{:S(2)}) async-start(f32[4,128,1024]{2,1,0:T(8,128)} %bitcast.3), calls=%async_computation | async-start | bytes 4194304 | tf_op jit(solution)/shard_map/all_to_all | solution.py:79
  209.3 4.3 %copy-start.9 = (s32[1,1,32]{2,1,0:T(1,128)S(1)}, s32[1,1,32]{2,1,0:T(1,128)}, u32[]{:S(2)}) copy-start(s32[1,1,32]{2,1,0:T(1,128)} %param.13) | copy-start | bytes 388
  209.3 4.2 %copy-start.10 = (s32[1,1,32]{2,1,0:T(1,128)S(1)}, s32[1,1,32]{2,1,0:T(1,128)}, u32[]{:S(2)}) copy-start(s32[1,1,32]{2,1,0:T(1,128)} %param.14) | copy-start | bytes 388
  210.7 41.8 %collective-permute-start.1 = (f32[768,512]{1,0:T(8,128)}, f32[768,512]{1,0:T(8,128)}, u32[]{:S(2)}, u32[]{:S(2)}) collective-permute-start(f32[768,512]{1,0:T(8,128)} %reshape.53), channel_id=1, source_target_pairs={{0,1},{1,0},{2,3},{3,2},{4,5},{5,4},{6,7},{7,6},{8,9},{9,8},{10,11... | collective-permute-start | bytes 4718600 | tf_op jit(solution)/shard_map/ppermute | solution.py:24
  234.7 17.8 %copy-start.2 = (f32[768,512]{1,0:T(8,128)S(1)}, f32[768,512]{1,0:T(8,128)}, u32[]{:S(2)}) copy-start(f32[768,512]{1,0:T(8,128)} %reshape.53) | copy-start | bytes 4718596
  234.7 19.7 %copy-start.6 = (f32[128,512]{1,0:T(8,128)}, f32[128,512]{1,0:T(8,128)S(1)}, u32[]{:S(2)}) copy-start(f32[128,512]{1,0:T(8,128)S(1)} %slice_negate_fusion) | copy-start | bytes 786436
  235.2 0.7 copy-start.7
  236.8 15.0 %all-to-all-start.5 = ((f32[32,1,512]{2,1,0:T(1,128)}), f32[32,1,512]{2,1,0:T(1,128)S(1)}, u32[]{:S(2)}, u32[]{:S(2)}) async-start(f32[32,1,512]{2,1,0:T(1,128)} %copy.21), calls=%async_computation.5 | async-start | bytes 131072 | tf_op jit(solution)/shard_map/all_to_all | solution.py:84
  252.5 2.1 copy-start.5
  254.7 1.0 copy-start.3
  255.8 3.2 %copy-start.4 = (f32[512,512]{1,0:T(8,128)}, f32[512,512]{1,0:T(8,128)S(1)}, u32[]{:S(2)}) copy-start(f32[512,512]{1,0:T(8,128)S(1)} %convolution_subtract_fusion) | copy-start | bytes 3145732
Sparse Core Ops, SparseCore 0:
  10.9 76.2 all-gather.1

commit v2 on v1

v2 whole, which is shorter than its diff:
```python
import functools

import jax
import jax.numpy as jnp
from jax import lax
from jax.experimental import pallas as pl
from jax.experimental.pallas import tpu as pltpu
from jax.sharding import Mesh, PartitionSpec as P

NIB = 8
IBR = 16
HIGH = lax.Precision.HIGH
HIGHEST = lax.Precision.HIGHEST
COL = ("y", "z", "core")
CHIPS = ("x", "y", "z")
F32 = jnp.float32
BF16 = jnp.bfloat16


def dot(left, right, left_dim=1, right_dim=0, precision=HIGH):
    return lax.dot_general(
        left,
        right,
        (((left_dim,), (right_dim,)), ((), ())),
        precision=precision,
        preferred_element_type=F32,
    )


def swap_core(value):
    return lax.ppermute(value, "core", [(0, 1), (1, 0)])


def hop(value, leg, step):
    pairs = []
    for y in range(4):
        for z in range(4):
            for core in range(2):
                along_z = core == leg
                to_y, to_z = (y, (z + step) % 4) if along_z else ((y + step) % 4, z)
                pairs.append((y * 8 + z * 2 + core, to_y * 8 + to_z * 2 + core))
    return lax.ppermute(value, COL, pairs)


def parts(value):
    high = value.astype(BF16)
    return high, (value - high.astype(F32)).astype(BF16)


def product_kernel(count, has_total, order, mine, other, *refs):
    pieces = refs[:count]
    out, piece_high, piece_low = refs[-3:]
    step = pl.program_id(0)
    core = order[pl.num_programs(0)]

    @pl.when(step == 0)
    def _():
        at = 0
        for piece in pieces:
            rows = piece.shape[0]
            piece_high[at : at + rows, :], piece_low[at : at + rows, :] = parts(piece[...])
            at += rows
        out[...] = refs[count][...] if has_total else jnp.zeros_like(out)

    at = pl.ds(pl.multiple_of(step * 256, 256), 256)
    high, low = piece_high[at, :], piece_low[at, :]
    right = jnp.concatenate([high, low, high], axis=0)
    for source, side in ((mine, core), (other, 1 - core)):
        top, rest = parts(source[...])
        left = jnp.concatenate([top, top, rest], axis=1)
        made = jnp.dot(left, right, preferred_element_type=F32)
        for row in range(4):
            to = pl.ds(pl.multiple_of(row * 256 + side * 128, 128), 128)
            out[to, :] += made[row * 128 : row * 128 + 128, :]


def add_product(order, mine, other, pieces, total=None):
    depth = sum(piece.shape[0] for piece in pieces)
    block = pl.BlockSpec((512, 256), lambda j, order: (0, order[j]))
    whole = [pl.BlockSpec(piece.shape, lambda j, order: (0, 0)) for piece in pieces]
    made = pl.BlockSpec((1024, 512), lambda j, order: (0, 0))
    has_total = total is not None
    args = [order, mine, other, *pieces] + ([total] if has_total else [])
    return pl.pallas_call(
        functools.partial(product_kernel, len(pieces), has_total),
        grid_spec=pltpu.PrefetchScalarGridSpec(
            num_scalar_prefetch=1,
            grid=(depth // 256,),
            in_specs=[block, block, *whole] + ([made] if has_total else []),
            out_specs=made,
            scratch_shapes=[pltpu.VMEM((depth, 512), BF16)] * 2,
        ),
        out_shape=jax.ShapeDtypeStruct((1024, 512), F32),
        cost_estimate=pl.CostEstimate(
            flops=6 * 1024 * 512 * depth, bytes_accessed=5120 * depth, transcendentals=0
        ),
    )(*args)


def gram_kernel(rows, z, out):
    rows_high, rows_low = parts(rows[...])
    z_high, z_low = parts(z[...])

    def product(left, right):
        return lax.dot_general(left, right, (((0,), (0,)), ((), ())), preferred_element_type=F32)

    def gram(at, to):
        return (
            product(rows_high[:, at], z_high[:, to])
            + product(rows_high[:, at], z_low[:, to])
            + product(rows_low[:, at], z_high[:, to])
        )

    @pl.when(pl.program_id(0) == 0)
    def _():
        out[...] = jnp.zeros_like(out)

    out[:, :512] += gram(slice(0, 512), slice(0, 512))
    out[:, 512:] += gram(slice(512, 1024), slice(256, 512))


def grams_of(rows, z):
    return pl.pallas_call(
        gram_kernel,
        grid=(4,),
        in_specs=[
            pl.BlockSpec((256, 1024), lambda k: (k, 0)),
            pl.BlockSpec((256, 512), lambda k: (k, 0)),
        ],
        out_specs=pl.BlockSpec((512, 768), lambda k: (0, 0)),
        out_shape=jax.ShapeDtypeStruct((512, 768), F32),
        cost_estimate=pl.CostEstimate(
            flops=6 * 1024 * 512 * 768, bytes_accessed=7 << 20, transcendentals=0
        ),
    )(rows, z)


def local(
    ancestor,
    panels,
    pattern,
    diag_inverse,
    link,
    block_list,
    gauge_owner,
    gauge_weight,
):
    row = lax.axis_index("x")
    place_y, place_z, core = (lax.axis_index(name) for name in COL)
    first = core == 0
    col = place_y * 8 + place_z * 2 + core
    flags = lax.dynamic_index_in_dim(pattern, col * 4 + row, 1, keepdims=False).astype(F32)
    tiles = panels.reshape(2, 128, 2, 256) * flags[:, None, :, None]
    left, right = tiles[:, :, 0], tiles[:, :, 1]
    theirs = swap_core(jnp.where(first, right, left))
    mine = jnp.where(first, left, right)
    own = jnp.concatenate([jnp.where(first, mine, theirs), jnp.where(first, theirs, mine)], axis=1)
    ancestor, theirs = lax.optimization_barrier((ancestor, theirs))
    other = swap_core(ancestor)

    def order_of(*offsets):
        order = []
        for leg_0, leg_1 in offsets:
            step_y = jnp.where(first, leg_1, leg_0)
            step_z = jnp.where(first, leg_0, leg_1)
            order.append(((place_y + step_y) % 4) * 4 + (place_z + step_z) % 4)
        return jnp.stack(order + [core]).astype(jnp.int32)

    both = jnp.concatenate([left[0], right[0], left[1], right[1]], axis=1)
    rows = lax.all_gather(both, ("x", "core"), axis=0, tiled=True)
    weights = jnp.broadcast_to(gauge_weight.reshape(1, 512), (8, 512))
    weights, rows = lax.optimization_barrier((weights, rows))
    weights = lax.all_gather(weights, COL, axis=0, tiled=True).reshape(32, 8, 512)[:, 0]
    weights = lax.dynamic_slice_in_dim(weights, col * IBR, IBR, axis=1)
    owner_match = (
        gauge_owner[0, 0][None, :] == jnp.arange(32, dtype=jnp.int32)[:, None]
    ).astype(F32)
    block_match = (
        block_list[0, 0][:, None] == jnp.arange(NIB, dtype=jnp.int32)[None, :]
    ).astype(F32)
    selector = dot(owner_match, block_match, precision=HIGHEST)
    combine = (selector[:, :, None] * weights[:, None, :]).reshape(32, NIB * IBR)
    own = jnp.concatenate([own[0], own[1]], axis=1)
    behind = hop(own, 0, 1)
    ahead = hop(own, 0, -1)
    across = hop(own, 0, 2)
    pair = jnp.concatenate([own, behind], axis=0)
    pair_behind = hop(pair, 1, 1)
    pair_ahead = hop(pair, 1, -1)
    rest = jnp.concatenate([ahead, across], axis=0)
    rest_behind = hop(rest, 1, 1)
    rest_ahead = hop(rest, 1, -1)
    z = add_product(order_of((0, 0), (-1, 0), (1, 0), (2, 0)), ancestor, other, (pair, rest))
    pair_behind, z = lax.optimization_barrier((pair_behind, z))
    pair_across = hop(pair_behind, 1, 1)
    z = add_product(
        order_of((0, -1), (-1, -1), (0, 1), (-1, 1)), ancestor, other, (pair_behind, pair_ahead), z
    )
    rest_ahead, z = lax.optimization_barrier((rest_ahead, z))
    rest_across = hop(rest_ahead, 1, -1)
    z = add_product(
        order_of((1, -1), (2, -1), (1, 1), (2, 1), (0, 2), (-1, 2)),
        ancestor,
        other,
        (rest_behind, rest_ahead, pair_across),
        z,
    )
    z, rows = lax.optimization_barrier((z, rows))
    z = add_product(order_of((1, 2), (2, 2)), ancestor, other, (rest_across,), z)

    z_pair = lax.psum_scatter(z, "x", scatter_dimension=0, tiled=True)
    grams = grams_of(rows, z)
    part = lax.all_to_all(grams.reshape(64, 8, 768), CHIPS, 0, 0, tiled=True).sum(0)

    z_mine = jnp.where(first, z_pair[:128], z_pair[128:])
    z_theirs = swap_core(jnp.where(first, z_pair[128:], z_pair[:128]))
    z_left = jnp.where(first, z_mine, z_theirs)
    z_right = jnp.where(first, z_theirs, z_mine)
    y_first = -jnp.concatenate([z_left[:, :256], z_right[:, :256]], axis=1)
    z_second = jnp.concatenate([z_left[:, 256:], z_right[:, 256:]], axis=1)
    y_second = -(z_second + dot(y_first, link))
    shares = dot(combine, y_second).reshape(1, 16, 8, 128)
    here = lax.broadcasted_iota(jnp.int32, (4, 1, 1, 1), 0) == row
    shares = jnp.where(here, shares, 0.0).reshape(64, 8, 128)
    message = jnp.concatenate([jnp.broadcast_to(part[None], (64, 8, 768)), shares], axis=2)
    message = lax.all_to_all(message, CHIPS, 0, 0, tiled=True)
    gauge = message[:, :, 768:].sum(0).reshape(2, 512)
    gauge = jnp.where(first, gauge[:1], gauge[1:]) + swap_core(
        jnp.where(first, gauge[1:], gauge[:1])
    )
    whole = message[:, :, :768].reshape(512, 768)
    others = swap_core(whole)
    left = jnp.where(first, whole, others)
    right = jnp.where(first, others, whole)

    def gram(slot):
        at = slice(slot * 256, slot * 256 + 256)
        return jnp.concatenate([left[:, at], right[:, at]], axis=1)

    diag_first = diag_inverse[0] + gram(0)
    cross = gram(1)
    cross_second = cross - dot(diag_first, link)
    diag_second = (
        diag_inverse[1] + gram(2) - dot(cross, link, 0, 0) - dot(link, cross_second, 0, 0)
    )
    return (y_first, diag_first, y_second, cross_second, diag_second, gauge.reshape(1, 1, 512))


def solution(mesh):
    grid = Mesh(mesh.devices.reshape(4, 4, 4, 2), CHIPS + ("core",))
    in_specs = (
        P(COL, "x"),
        P(None, COL + ("x",), None),
        P(),
        P(),
        P(),
        P(COL, "x", None),
        P(COL, "x", None),
        P("x", COL, None),
    )
    out_specs = (
        P(COL + ("x",), None),
        P(),
        P(COL + ("x",), None),
        P(),
        P(),
        P("x", COL, None),
    )
    return jax.shard_map(local, mesh=grid, in_specs=in_specs, out_specs=out_specs, check_vma=False)
```

time: 267 us -> 193 us (0.72)
  waiting for transfers between devices: 132 us -> 21.6 us
  Pallas kernels: 0 us -> 43.9 us
  blocking collectives: 32.3 us -> 64.7 us
  matrix products: 31.3 us -> 5.09 us
  other arithmetic: 10.8 us -> 5.32 us
  local copies, waits for them, and re-layouts: 10.4 us -> 5.86 us
  starting transfers between devices: 35.1 us -> 31.7 us
    all_gather x1, waiting for transfers between devices: 69.4 us -> 0.01 us  [local(): rows = lax.all_gather(both, ('x', 'core'), axis=0, tiled=True)]
    all_to_all x5 -> x1, waiting for transfers between devices: 58.9 us -> 0.01 us  [local(): lax.all_to_all(grams.reshape(64, 8, 768), CHIPS, 0, 0, tiled=True).sum(0)]
    pallas_call x0 -> x5, Pallas kernels: none -> 43.9 us  [the longest x4 36.5 us: add_product(): pl.pallas_call(functools.partial(product_kernel, len(pieces), has_total),...]
    all_gather x0 -> x1, blocking collectives: none -> 29 us  [local(): lax.all_gather(weights, COL, axis=0, tiled=True).reshape(32, 8, 512)[:, 0]]
    dot_general x10 -> x6, matrix products: 31.3 us -> 5.09 us  [dot(): lax.dot_general(left, right, (((left_dim,), (right_dim,)), ((), ())), pre...]
    all_to_all x5 -> x1, starting transfers between devices: 31.7 us -> 10 us  [local(): lax.all_to_all(grams.reshape(64, 8, 768), CHIPS, 0, 0, tiled=True).sum(0)]
    ppermute x0 -> x9, starting transfers between devices: none -> 16 us  [hop(): return lax.ppermute(value, COL, pairs)]
    ppermute x0 -> x9, waiting for transfers between devices: none -> 15.2 us  [hop(): return lax.ppermute(value, COL, pairs)]
  transfers between devices with their start and end apart: 8 -> 17, of which waited for: 6 -> 8; matrix products, arithmetic and copies ran while one was open for 11% -> 4% of each run, Pallas kernels for 0% -> 19%
where the time goes in v2:
time: 193 us
  blocking collectives  64.7 us (34%)
  Pallas kernels  43.9 us (23%)
  starting transfers between devices  31.7 us (16%)
  waiting for transfers between devices  21.6 us (11%)
  between operations  14.6 us (8%)
  local copies, waits for them, and re-layouts  5.86 us (3%)
  other arithmetic  5.32 us (3%)
  matrix products  5.09 us (3%)
    pallas_call x4, Pallas kernels, add_product(): pl.pallas_call(functools.partial(product_kernel, len(pieces), has_total),...  36.5 us
    all_to_all x1, blocking collectives, local(): message = lax.all_to_all(message, CHIPS, 0, 0, tiled=True)  35.7 us
    all_gather x1, blocking collectives, local(): lax.all_gather(weights, COL, axis=0, tiled=True).reshape(32, 8, 512)[:, 0]  29 us
    ppermute x9, starting transfers between devices, hop(): return lax.ppermute(value, COL, pairs)  16 us
    ppermute x9, waiting for transfers between devices, hop(): return lax.ppermute(value, COL, pairs)  15.2 us
    all_to_all x1, starting transfers between devices, local(): lax.all_to_all(grams.reshape(64, 8, 768), CHIPS, 0, 0, tiled=True).sum(0)  10 us
    pallas_call x1, Pallas kernels, grams_of(): pl.pallas_call(gram_kernel, grid=(4,), in_specs=[pl.BlockSpec((256, 1024)...  7.36 us
    ppermute x5, starting transfers between devices, swap_core(): return lax.ppermute(value, 'core', [(0, 1), (1, 0)])  5.59 us
  transfers between devices with their start and end apart: 17, of which 8 were waited for; matrix products, arithmetic and copies ran while one was open for 4% of the time, Pallas kernels for 19%

profile of v2, /device:TPU:1, one launch (start us, length us, event | category | flops | bytes accessed | tf_op | source)
XLA Modules:
  0.0 192.7 jit_solution(17519930811345912475)
XLA Ops:
  9.1 1.5 collective-permute-start
  13.3 1.4 collective-permute-start.5
  14.7 1.5 collective-permute-start.2
  16.2 1.6 collective-permute-start.3
  17.8 5.2 %collective-permute-done.5 = f32[256,512]{1,0:T(8,128)S(1)} collective-permute-done((f32[256,512]{1,0:T(8,128)S(1)}, f32[256,512]{1,0:T(8,128)S(1)}, u32[]{:S(2)}, u32[]{:S(2)}) %collective-permute-start.5) | collective-permute-done | bytes 524320 | tf_op jit(solution)/shard_map/ppermute | solution.py:42
  23.1 1.4 collective-permute-start.6
  24.6 2.5 %collective-permute-start.7 = (f32[512,512]{1,0:T(8,128)S(1)}, f32[512,512]{1,0:T(8,128)}, u32[]{:S(2)}, u32[]{:S(2)}) collective-permute-start(f32[512,512]{1,0:T(8,128)S(1)} %pad_maximum_fusion.1.refs_0_), channel_id=1, source_target_pairs={{0,24},{1,7},{2,26},{3,1},{4,28},{5,3},{6,30},{7,5},{8,0},{9,15},{... | collective-permute-start | bytes 3145736 | tf_op jit(solution)/shard_map/ppermute | solution.py:42
  28.0 1.8 collective-permute-done.3
  29.9 4.9 %collective-permute-start.4 = (f32[512,512]{1,0:T(8,128)S(1)}, f32[512,512]{1,0:T(8,128)}, u32[]{:S(2)}, u32[]{:S(2)}) collective-permute-start(f32[512,512]{1,0:T(8,128)S(1)} %constant_dynamic-update-slice_fusion.refs_1_), channel_id=1, source_target_pairs={{0,24},{1,7},{2,26},{3,1},{4,28},{5,3},{6,30},{7,5},{8,0},{9,15},{... | collective-permute-start | bytes 3145736 | tf_op jit(solution)/shard_map/ppermute | solution.py:42
  35.4 8.7 %shard_map.127.refs_2_ = f32[1024,512]{1,0:T(8,128)} custom-call(s32[5]{0:T(128)} %stack.79.order, f32[512,4096]{1,0:T(8,128)} %mine.3, f32[512,4096]{1,0:T(8,128)} %collective-permute-done.1.other, f32[512,512]{1,0:T(8,128)} %copy-done.1, f32[512,512]{1,0:T(8,128)} %copy-done.4), custom_call_target="tpu_custom_call" | custom-call | flops 3221225472 | bytes 5242880 | tf_op jit(solution)/shard_map/pallas_call | solution.py:84
  44.8 9.4 %shard_map.128.refs_3_ = f32[1024,512]{1,0:T(8,128)} custom-call(s32[5]{0:T(128)} %stack.74.order, f32[512,4096]{1,0:T(8,128)} %mine.3, f32[512,4096]{1,0:T(8,128)} %collective-permute-done.1.other, f32[512,512]{1,0:T(8,128)} %collective-permute-done.6.refs_0_, f32[512,512]{1,0:T(8,128)} %collective-permute-done.7.refs_1_, f32[1024,512]{1,0:T(8,128)} %shard_map.127.refs_2_), custom_call_target="tpu_custom_call" | custom-call | flops 3221225472 | bytes 5242880 | tf_op jit(solution)/shard_map/pallas_call | solution.py:84
  54.2 2.7 %collective-permute-start.8 = (f32[512,512]{1,0:T(8,128)}, f32[512,512]{1,0:T(8,128)S(1)}, u32[]{:S(2)}, u32[]{:S(2)}) collective-permute-start(f32[512,512]{1,0:T(8,128)} %collective-permute-done.4.refs_1_), channel_id=1, source_target_pairs={{0,24},{1,7},{2,26},{3,1},{4,28},{5,3},{6,30},{7,5},{8,0},{9,15},{... | collective-permute-start | bytes 3145736 | tf_op jit(solution)/shard_map/ppermute | solution.py:42
  58.0 7.2 %collective-permute-done.10.refs_2_ = f32[512,512]{1,0:T(8,128)} collective-permute-done((f32[512,512]{1,0:T(8,128)}, f32[512,512]{1,0:T(8,128)}, u32[]{:S(2)}, u32[]{:S(2)}) %collective-permute-start.10) | collective-permute-done | bytes 1048608 | tf_op jit(solution)/shard_map/ppermute | solution.py:42
  65.3 11.9 %shard_map.129.refs_1_ = f32[1024,512]{1,0:T(8,128)} custom-call(s32[7]{0:T(128)} %stack.86.order, f32[512,4096]{1,0:T(8,128)} %mine.3, f32[512,4096]{1,0:T(8,128)} %collective-permute-done.1.other, f32[512,512]{1,0:T(8,128)} %collective-permute-done.9.refs_0_, f32[512,512]{1,0:T(8,128)} %collective-permute-done.4.refs_1_, ...), custom_call_target="tpu_custom_call" | custom-call | flops 4831838208 | bytes 7864320 | tf_op jit(solution)/shard_map/pallas_call | solution.py:84
  78.2 6.5 %shard_map.130.z = f32[1024,512]{1,0:T(8,128)} custom-call(s32[3]{0:T(128)} %pad_add_fusion.order, f32[512,4096]{1,0:T(8,128)} %mine.3, f32[512,4096]{1,0:T(8,128)} %collective-permute-done.1.other, f32[512,512]{1,0:T(8,128)} %copy-done.7, f32[1024,512]{1,0:T(8,128)} %shard_map.129.refs_1_), custom_call_target="tpu_custom_call" | custom-call | flops 1610612736 | bytes 2621440 | tf_op jit(solution)/shard_map/pallas_call | solution.py:84
  84.7 7.4 %shard_map.131 = f32[512,768]{1,0:T(8,128)} custom-call(f32[1024,1024]{1,0:T(8,128)} %all-gather.2.cloned.1.call-done.rows, f32[1024,512]{1,0:T(8,128)} %shard_map.130.z), custom_call_target="tpu_custom_call" | custom-call | flops 2415919104 | bytes 7340032 | tf_op jit(solution)/shard_map/pallas_call | solution.py:123
  92.1 10.0 %all-to-all-start = ((f32[64,8,768]{2,1,0:T(8,128)}), f32[64,8,768]{2,1,0:T(8,128)S(1)}, u32[]{:S(2)}, u32[]{:S(2)}) async-start(f32[64,8,768]{2,1,0:T(8,128)} %bitcast.86), calls=%async_computation.1 | async-start | bytes 3145728 | tf_op jit(solution)/shard_map/all_to_all | solution.py:213
  102.5 29.0 %all_gather.7 = f32[256,512]{1,0:T(8,128)S(1)} all-gather(f32[8,512]{1,0:T(8,128)S(1)} %broadcast_in_dim.47), channel_id=1, replica_groups=mesh['x'=4,'y'=4,'z'=4,'core'=2] {'y','z','core'}, dimensions={0}, use_global_device_ids=true | all-gather | bytes 540672 | tf_op jit(solution)/shard_map/all_gather | solution.py:173
  131.6 1.3 reduce-scatter.2.cloned.1.call-done
  132.9 1.8 slice_select_fusion
  138.2 35.7 %all_to_all.10 = f32[64,8,896]{2,1,0:T(8,128)S(1)} all-to-all(f32[64,8,896]{2,1,0:T(8,128)S(1)} %pad_maximum_fusion), channel_id=1, replica_groups=mesh['x'=4,'y'=4,'z'=4,'core'=2] {'x','y','z'}, dimensions={0} | all-to-all | bytes 3670016 | tf_op jit(solution)/shard_map/all_to_all | solution.py:226
  174.1 2.8 %collective-permute-start.12 = (f32[512,768]{1,0:T(8,128)S(1)}, f32[512,768]{1,0:T(8,128)S(1)}, u32[]{:S(2)}, u32[]{:S(2)}) collective-permute-start(f32[512,768]{1,0:T(8,128)S(1)} %slice_bitcast_fusion), channel_id=1, source_target_pairs={{0,1},{1,0},{2,3},{3,2},{4,5},{5,4},{6,7},{7,6},{8,9},{9,8},{10,11... | collective-permute-start | bytes 4718600 | tf_op jit(solution)/shard_map/ppermute | solution.py:31
  177.0 2.9 %collective-permute-done.13 = f32[1,512]{1,0:T(1,128)S(1)} collective-permute-done((f32[1,512]{1,0:T(1,128)S(1)}, f32[1,512]{1,0:T(1,128)S(1)}, u32[]{:S(2)}, u32[]{:S(2)}) %collective-permute-start.13) | collective-permute-done | bytes 2080 | tf_op jit(solution)/shard_map/ppermute | solution.py:31
  183.8 2.1 %fusion = f32[512,512]{1,0:T(8,128)} fusion(f32[512,512]{1,0:T(8,128)S(1)} %convolution_subtract_fusion, f32[512,512]{1,0:T(8,128)S(1)} %copy-done, f32[512,512]{1,0:T(8,128)S(1)} %fusion.2, f32[512,256]{1,0:T(8,128)S(1)} %get-tuple-element.29, f32[512,256]{1,0:T(8,128)S(1)} %get-tuple-element.26, f32[2,512,512]{2,1,0:T(8,128)S(1)} %copy-done.6), kind=kOutput, calls=%fused_computation.3 | convolution fusion | flops 806354944 | bytes 6291456 | tf_op jit(solution)/shard_map/dot_general | solution.py:21
  (95 shorter events, 16.9 us)
Async XLA Ops:
  7.2 129.9 %copy-start = (f32[512,512]{1,0:T(8,128)S(1)}, f32[512,512]{1,0:T(8,128)}, u32[]{:S(2)}) copy-start(f32[512,512]{1,0:T(8,128)} %param.12) | copy-start | bytes 3145732
  7.2 50.8 %all-gather.2.cloned.1.call-start = ((), (), s32[]{:S(2)}) async-start(), calls=%async_computation.3 | async-start | bytes 4718592 | tf_op jit(solution)/shard_map/all_gather | solution.py:170
  9.1 2.7 %collective-permute-start = (f32[2,128,256]{2,1,0:T(8,128)S(1)}, f32[2,128,256]{2,1,0:T(8,128)S(1)}, u32[]{:S(2)}, u32[]{:S(2)}) collective-permute-start(f32[2,128,256]{2,1,0:T(8,128)S(1)} %fusion.7), channel_id=1, source_target_pairs={{0,1},{1,0},{2,3},{3,2},{4,5},{5,4},{6,7},{7,6},{8,9},{9,8},{10,11... | collective-permute-start | bytes 786440 | tf_op jit(solution)/shard_map/ppermute | solution.py:31
  11.8 23.6 %collective-permute-start.1 = (f32[512,4096]{1,0:T(8,128)}, f32[512,4096]{1,0:T(8,128)}, u32[]{:S(2)}, u32[]{:S(2)}) collective-permute-start(f32[512,4096]{1,0:T(8,128)} %mine.3), channel_id=1, source_target_pairs={{0,1},{1,0},{2,3},{3,2},{4,5},{5,4},{6,7},{7,6},{8,9},{9,8},{10,11... | collective-permute-start | bytes 25165832 | tf_op jit(solution)/shard_map/ppermute | solution.py:31
  13.1 119.8 %reduce-scatter.2.cloned.1.call-start = ((), (), s32[]{:S(2)}) async-start(), calls=%async_computation.4 | async-start | bytes 2621440 | tf_op jit(solution)/shard_map/reduce_scatter | solution.py:211
  13.3 9.8 %collective-permute-start.5 = (f32[256,512]{1,0:T(8,128)S(1)}, f32[256,512]{1,0:T(8,128)S(1)}, u32[]{:S(2)}, u32[]{:S(2)}) collective-permute-start(f32[256,512]{1,0:T(8,128)S(1)} %pad_maximum_fusion.4), channel_id=1, source_target_pairs={{0,2},{1,9},{2,4},{3,11},{4,6},{5,13},{6,0},{7,15},{8,10},{9,17},{... | collective-permute-start | bytes 1572872 | tf_op jit(solution)/shard_map/ppermute | solution.py:42
  14.7 13.3 %collective-permute-start.2 = (f32[256,512]{1,0:T(8,128)S(1)}, f32[256,512]{1,0:T(8,128)S(1)}, u32[]{:S(2)}, u32[]{:S(2)}) collective-permute-start(f32[256,512]{1,0:T(8,128)S(1)} %pad_maximum_fusion.4), channel_id=1, source_target_pairs={{0,6},{1,25},{2,0},{3,27},{4,2},{5,29},{6,4},{7,31},{8,14},{9,1},{... | collective-permute-start | bytes 1572872 | tf_op jit(solution)/shard_map/ppermute | solution.py:42
  16.2 13.6 %collective-permute-start.3 = (f32[256,512]{1,0:T(8,128)S(1)}, f32[256,512]{1,0:T(8,128)S(1)}, u32[]{:S(2)}, u32[]{:S(2)}) collective-permute-start(f32[256,512]{1,0:T(8,128)S(1)} %pad_maximum_fusion.4), channel_id=1, source_target_pairs={{0,4},{1,17},{2,6},{3,19},{4,0},{5,21},{6,2},{7,23},{8,12},{9,25},... | collective-permute-start | bytes 1572872 | tf_op jit(solution)/shard_map/ppermute | solution.py:42
  23.1 12.2 %copy-start.1 = (f32[512,512]{1,0:T(8,128)}, f32[512,512]{1,0:T(8,128)S(1)}, u32[]{:S(2)}) copy-start(f32[512,512]{1,0:T(8,128)S(1)} %pad_maximum_fusion.1.refs_0_) | copy-start | bytes 3145732
  23.1 20.9 %collective-permute-start.6 = (f32[512,512]{1,0:T(8,128)S(1)}, f32[512,512]{1,0:T(8,128)}, u32[]{:S(2)}, u32[]{:S(2)}) collective-permute-start(f32[512,512]{1,0:T(8,128)S(1)} %pad_maximum_fusion.1.refs_0_), channel_id=1, source_target_pairs={{0,8},{1,3},{2,10},{3,5},{4,12},{5,7},{6,14},{7,1},{8,16},{9,11},{... | collective-permute-start | bytes 3145736 | tf_op jit(solution)/shard_map/ppermute | solution.py:42
  24.6 20.2 %collective-permute-start.7 = (f32[512,512]{1,0:T(8,128)S(1)}, f32[512,512]{1,0:T(8,128)}, u32[]{:S(2)}, u32[]{:S(2)}) collective-permute-start(f32[512,512]{1,0:T(8,128)S(1)} %pad_maximum_fusion.1.refs_0_), channel_id=1, source_target_pairs={{0,24},{1,7},{2,26},{3,1},{4,28},{5,3},{6,30},{7,5},{8,0},{9,15},{... | collective-permute-start | bytes 3145736 | tf_op jit(solution)/shard_map/ppermute | solution.py:42
  29.9 5.5 %copy-start.4 = (f32[512,512]{1,0:T(8,128)}, f32[512,512]{1,0:T(8,128)S(1)}, u32[]{:S(2)}) copy-start(f32[512,512]{1,0:T(8,128)S(1)} %constant_dynamic-update-slice_fusion.refs_1_) | copy-start | bytes 3145732
  29.9 24.3 %collective-permute-start.4 = (f32[512,512]{1,0:T(8,128)S(1)}, f32[512,512]{1,0:T(8,128)}, u32[]{:S(2)}, u32[]{:S(2)}) collective-permute-start(f32[512,512]{1,0:T(8,128)S(1)} %constant_dynamic-update-slice_fusion.refs_1_), channel_id=1, source_target_pairs={{0,24},{1,7},{2,26},{3,1},{4,28},{5,3},{6,30},{7,5},{8,0},{9,15},{... | collective-permute-start | bytes 3145736 | tf_op jit(solution)/shard_map/ppermute | solution.py:42
  35.3 22.7 %collective-permute-start.9 = (f32[512,512]{1,0:T(8,128)S(1)}, f32[512,512]{1,0:T(8,128)}, u32[]{:S(2)}, u32[]{:S(2)}) collective-permute-start(f32[512,512]{1,0:T(8,128)S(1)} %constant_dynamic-update-slice_fusion.refs_1_), channel_id=1, source_target_pairs={{0,8},{1,3},{2,10},{3,5},{4,12},{5,7},{6,14},{7,1},{8,16},{9,11},{... | collective-permute-start | bytes 3145736 | tf_op jit(solution)/shard_map/ppermute | solution.py:42
  44.0 21.2 %collective-permute-start.10 = (f32[512,512]{1,0:T(8,128)}, f32[512,512]{1,0:T(8,128)}, u32[]{:S(2)}, u32[]{:S(2)}) collective-permute-start(f32[512,512]{1,0:T(8,128)} %collective-permute-done.6.refs_0_), channel_id=1, source_target_pairs={{0,8},{1,3},{2,10},{3,5},{4,12},{5,7},{6,14},{7,1},{8,16},{9,11},{... | collective-permute-start | bytes 3145736 | tf_op jit(solution)/shard_map/ppermute | solution.py:42
  44.8 13.3 %copy-start.10 = (f32[1,1,512]{2,1,0:T(1,128)S(1)}, f32[1,1,512]{2,1,0:T(1,128)}, u32[]{:S(2)}) copy-start(f32[1,1,512]{2,1,0:T(1,128)} %param.15) | copy-start | bytes 6148
  54.2 23.0 %collective-permute-start.8 = (f32[512,512]{1,0:T(8,128)}, f32[512,512]{1,0:T(8,128)S(1)}, u32[]{:S(2)}, u32[]{:S(2)}) collective-permute-start(f32[512,512]{1,0:T(8,128)} %collective-permute-done.4.refs_1_), channel_id=1, source_target_pairs={{0,24},{1,7},{2,26},{3,1},{4,28},{5,3},{6,30},{7,5},{8,0},{9,15},{... | collective-permute-start | bytes 3145736 | tf_op jit(solution)/shard_map/ppermute | solution.py:42
  92.1 10.2 %copy-start.12 = (s32[1,1,32]{2,1,0:T(1,128)S(1)}, s32[1,1,32]{2,1,0:T(1,128)}, u32[]{:S(2)}) copy-start(s32[1,1,32]{2,1,0:T(1,128)} %param.13) | copy-start | bytes 388
  92.1 10.2 %copy-start.13 = (s32[1,1,32]{2,1,0:T(1,128)S(1)}, s32[1,1,32]{2,1,0:T(1,128)}, u32[]{:S(2)}) copy-start(s32[1,1,32]{2,1,0:T(1,128)} %param.14) | copy-start | bytes 388
  92.1 43.7 %all-to-all-start = ((f32[64,8,768]{2,1,0:T(8,128)}), f32[64,8,768]{2,1,0:T(8,128)S(1)}, u32[]{:S(2)}, u32[]{:S(2)}) async-start(f32[64,8,768]{2,1,0:T(8,128)} %bitcast.86), calls=%async_computation.1 | async-start | bytes 3145728 | tf_op jit(solution)/shard_map/all_to_all | solution.py:213
  132.9 4.0 %copy-start.5 = (f32[256,512]{1,0:T(8,128)S(1)}, f32[256,512]{1,0:T(8,128)}, u32[]{:S(2)}) copy-start(f32[256,512]{1,0:T(8,128)} %reduce-scatter.2.cloned.1.call-done) | copy-start | bytes 1572868
  134.7 2.2 %collective-permute-start.11 = (f32[128,512]{1,0:T(8,128)}, f32[128,512]{1,0:T(8,128)S(1)}, u32[]{:S(2)}, u32[]{:S(2)}) collective-permute-start(f32[128,512]{1,0:T(8,128)} %slice_select_fusion), channel_id=1, source_target_pairs={{0,1},{1,0},{2,3},{3,2},{4,5},{5,4},{6,7},{7,6},{8,9},{9,8},{10,11... | collective-permute-start | bytes 786440 | tf_op jit(solution)/shard_map/ppermute | solution.py:31
  174.1 6.4 %collective-permute-start.12 = (f32[512,768]{1,0:T(8,128)S(1)}, f32[512,768]{1,0:T(8,128)S(1)}, u32[]{:S(2)}, u32[]{:S(2)}) collective-permute-start(f32[512,768]{1,0:T(8,128)S(1)} %slice_bitcast_fusion), channel_id=1, source_target_pairs={{0,1},{1,0},{2,3},{3,2},{4,5},{5,4},{6,7},{7,6},{8,9},{9,8},{10,11... | collective-permute-start | bytes 4718600 | tf_op jit(solution)/shard_map/ppermute | solution.py:31
  176.9 3.0 %collective-permute-start.13 = (f32[1,512]{1,0:T(1,128)S(1)}, f32[1,512]{1,0:T(1,128)S(1)}, u32[]{:S(2)}, u32[]{:S(2)}) collective-permute-start(f32[1,512]{1,0:T(1,128)S(1)} %bitcast.92), channel_id=1, source_target_pairs={{0,1},{1,0},{2,3},{3,2},{4,5},{5,4},{6,7},{7,6},{8,9},{9,8},{10,11... | collective-permute-start | bytes 6152 | tf_op jit(solution)/shard_map/ppermute | solution.py:31
  (7 other events, 9.0 us)
Sparse Core Ops, SparseCore 0:
  13.2 34.4 all-gather.1
  84.8 48.0 reduce-scatter.1

commit v3 on v2

--- a/solution.py
+++ b/solution.py
@@ -97,42 +97,107 @@
     )(*args)
 
 
-def gram_kernel(rows, z, out):
+def gram_kernel(core, rows, z, out):
     rows_high, rows_low = parts(rows[...])
     z_high, z_low = parts(z[...])
+    first = core[0] == 0
 
     def product(left, right):
-        return lax.dot_general(left, right, (((0,), (0,)), ((), ())), preferred_element_type=F32)
-
-    def gram(at, to):
-        return (
-            product(rows_high[:, at], z_high[:, to])
-            + product(rows_high[:, at], z_low[:, to])
-            + product(rows_low[:, at], z_high[:, to])
-        )
+        def terms(one, two):
+            return lax.dot_general(one, two, (((0,), (0,)), ((), ())), preferred_element_type=F32)
+
+        return terms(left[0], right[0]) + terms(left[0], right[1]) + terms(left[1], right[0])
+
+    def panel(start, stop):
+        return rows_high[:, start:stop], rows_low[:, start:stop]
+
+    def kept(start, stop):
+        return z_high[:, start:stop], z_low[:, start:stop]
+
+    def either(one, two):
+        return tuple(jnp.where(first, left, right) for left, right in zip(one, two))
 
     @pl.when(pl.program_id(0) == 0)
     def _():
         out[...] = jnp.zeros_like(out)
 
-    out[:, :512] += gram(slice(0, 512), slice(0, 512))
-    out[:, 512:] += gram(slice(512, 1024), slice(256, 512))
-
-
-def grams_of(rows, z):
+    out[:, :256] += product(panel(0, 512), kept(256, 512))
+    for slot in range(2):
+        at, start, half = slice(slot * 256, slot * 256 + 256), slot * 512, slot * 256
+        low, high = panel(start, start + 256), panel(start + 256, start + 512)
+        mine = kept(half, half + 256)
+        out[at, 256:512] += product(either(low, high), mine)
+        out[at, 512:] += product(
+            either(high, mine), either(kept(half, half + 128), panel(start + 128, start + 256))
+        )
+
+
+def grams_of(core, rows, z):
     return pl.pallas_call(
         gram_kernel,
-        grid=(4,),
-        in_specs=[
-            pl.BlockSpec((256, 1024), lambda k: (k, 0)),
-            pl.BlockSpec((256, 512), lambda k: (k, 0)),
-        ],
-        out_specs=pl.BlockSpec((512, 768), lambda k: (0, 0)),
-        out_shape=jax.ShapeDtypeStruct((512, 768), F32),
+        grid_spec=pltpu.PrefetchScalarGridSpec(
+            num_scalar_prefetch=1,
+            grid=(4,),
+            in_specs=[
+                pl.BlockSpec((256, 1024), lambda k, core: (k, 0)),
+                pl.BlockSpec((256, 512), lambda k, core: (k, 0)),
+            ],
+            out_specs=pl.BlockSpec((512, 640), lambda k, core: (0, 0)),
+        ),
+        out_shape=jax.ShapeDtypeStruct((512, 640), F32),
         cost_estimate=pl.CostEstimate(
-            flops=6 * 1024 * 512 * 768, bytes_accessed=7 << 20, transcendentals=0
-        ),
-    )(rows, z)
+            flops=6 * 1024 * 512 * 640, bytes_accessed=7 << 20, transcendentals=0
+        ),
+    )(core, rows, z)
+
+
+def close_kernel(core, mine, theirs, diag, link, diag_first, cross_second, diag_second):
+    first = core[0] == 0
+
+    def sides(rows, columns):
+        kept, came = mine[rows, columns], theirs[rows, columns]
+        return jnp.where(first, kept, came), jnp.where(first, came, kept)
+
+    def symmetric(slot):
+        rows = slice(slot * 256, slot * 256 + 256)
+        upper, lower = sides(rows, slice(256, 512))
+        below = jnp.concatenate(sides(rows, slice(512, 640)), axis=1)
+        return jnp.concatenate(
+            [
+                jnp.concatenate([upper, below.T], axis=1),
+                jnp.concatenate([below, lower], axis=1),
+            ],
+            axis=0,
+        )
+
+    def product(left, right, dim=1):
+        def terms(one, two):
+            return lax.dot_general(one, two, (((dim,), (0,)), ((), ())), preferred_element_type=F32)
+
+        left, right = parts(left), parts(right)
+        return terms(left[0], right[0]) + terms(left[0], right[1]) + terms(left[1], right[0])
+
+    cross = jnp.concatenate(sides(slice(0, 512), slice(0, 256)), axis=1)
+    links = link[...]
+    top = diag[0] + symmetric(0)
+    diag_first[...] = top
+    second = cross - product(top, links)
+    cross_second[...] = second
+    diag_second[...] = (
+        diag[1] + symmetric(1) - product(cross, links, 0) - product(links, second, 0)
+    )
+
+
+def close(core, mine, theirs, diag, link):
+    return pl.pallas_call(
+        close_kernel,
+        in_specs=[pl.BlockSpec(memory_space=pltpu.SMEM)]
+        + [pl.BlockSpec(memory_space=pltpu.VMEM)] * 4,
+        out_shape=[jax.ShapeDtypeStruct((512, 512), F32)] * 3,
+        cost_estimate=pl.CostEstimate(
+            flops=36 * 512 * 512 * 512, bytes_accessed=9 << 20, transcendentals=0
+        ),
+    )(core, mine, theirs, diag, link)
 
 
 def local(
@@ -168,22 +233,14 @@
 
     both = jnp.concatenate([left[0], right[0], left[1], right[1]], axis=1)
     rows = lax.all_gather(both, ("x", "core"), axis=0, tiled=True)
-    weights = jnp.broadcast_to(gauge_weight.reshape(1, 512), (8, 512))
-    weights, rows = lax.optimization_barrier((weights, rows))
-    weights = lax.all_gather(weights, COL, axis=0, tiled=True).reshape(32, 8, 512)[:, 0]
-    weights = lax.dynamic_slice_in_dim(weights, col * IBR, IBR, axis=1)
-    owner_match = (
-        gauge_owner[0, 0][None, :] == jnp.arange(32, dtype=jnp.int32)[:, None]
-    ).astype(F32)
-    block_match = (
-        block_list[0, 0][:, None] == jnp.arange(NIB, dtype=jnp.int32)[None, :]
-    ).astype(F32)
-    selector = dot(owner_match, block_match, precision=HIGHEST)
-    combine = (selector[:, :, None] * weights[:, None, :]).reshape(32, NIB * IBR)
     own = jnp.concatenate([own[0], own[1]], axis=1)
     behind = hop(own, 0, 1)
     ahead = hop(own, 0, -1)
     across = hop(own, 0, 2)
+    weights = jnp.broadcast_to(gauge_weight.reshape(1, 512), (16, 512))
+    weights, behind = lax.optimization_barrier((weights, behind))
+    weights = lax.all_gather(weights, COL, axis=0, tiled=True).reshape(32, 16, 512)[:, 0]
+    weights = lax.dynamic_slice_in_dim(weights, col * IBR, IBR, axis=1)
     pair = jnp.concatenate([own, behind], axis=0)
     pair_behind = hop(pair, 1, 1)
     pair_ahead = hop(pair, 1, -1)
@@ -208,9 +265,21 @@
     z, rows = lax.optimization_barrier((z, rows))
     z = add_product(order_of((1, 2), (2, 2)), ancestor, other, (rest_across,), z)
 
+    owner_match = (
+        gauge_owner[0, 0][None, :] == jnp.arange(32, dtype=jnp.int32)[:, None]
+    ).astype(F32)
+    block_match = (
+        block_list[0, 0][:, None] == jnp.arange(NIB, dtype=jnp.int32)[None, :]
+    ).astype(F32)
+    selector = dot(owner_match, block_match, precision=HIGHEST)
+    combine = (selector[:, :, None] * weights[:, None, :]).reshape(32, NIB * IBR)
+    core_list = core.astype(jnp.int32).reshape(1)
+    plane = ("y", "z")
     z_pair = lax.psum_scatter(z, "x", scatter_dimension=0, tiled=True)
-    grams = grams_of(rows, z)
-    part = lax.all_to_all(grams.reshape(64, 8, 768), CHIPS, 0, 0, tiled=True).sum(0)
+    part = grams_of(core_list, rows, z).reshape(16, 32, 640)
+    part = lax.all_to_all(part, plane, 0, 0, tiled=True).sum(0)
+    part = jnp.broadcast_to(part[None], (4, 32, 640))
+    part = lax.all_to_all(part, "x", 0, 0, tiled=True).sum(0)
 
     z_mine = jnp.where(first, z_pair[:128], z_pair[128:])
     z_theirs = swap_core(jnp.where(first, z_pair[128:], z_pair[:128]))
@@ -219,29 +288,16 @@
     y_first = -jnp.concatenate([z_left[:, :256], z_right[:, :256]], axis=1)
     z_second = jnp.concatenate([z_left[:, 256:], z_right[:, 256:]], axis=1)
     y_second = -(z_second + dot(y_first, link))
-    shares = dot(combine, y_second).reshape(1, 16, 8, 128)
-    here = lax.broadcasted_iota(jnp.int32, (4, 1, 1, 1), 0) == row
-    shares = jnp.where(here, shares, 0.0).reshape(64, 8, 128)
-    message = jnp.concatenate([jnp.broadcast_to(part[None], (64, 8, 768)), shares], axis=2)
-    message = lax.all_to_all(message, CHIPS, 0, 0, tiled=True)
-    gauge = message[:, :, 768:].sum(0).reshape(2, 512)
+    shares = jnp.pad(dot(combine, y_second).reshape(16, 8, 128), ((0, 0), (0, 24), (0, 0)))
+    message = jnp.concatenate([jnp.broadcast_to(part[None], (16, 32, 640)), shares], axis=2)
+    message = lax.all_to_all(message, plane, 0, 0, tiled=True)
+    gauge = message[:, :8, 640:].sum(0).reshape(2, 512)
     gauge = jnp.where(first, gauge[:1], gauge[1:]) + swap_core(
         jnp.where(first, gauge[1:], gauge[:1])
     )
-    whole = message[:, :, :768].reshape(512, 768)
-    others = swap_core(whole)
-    left = jnp.where(first, whole, others)
-    right = jnp.where(first, others, whole)
-
-    def gram(slot):
-        at = slice(slot * 256, slot * 256 + 256)
-        return jnp.concatenate([left[:, at], right[:, at]], axis=1)
-
-    diag_first = diag_inverse[0] + gram(0)
-    cross = gram(1)
-    cross_second = cross - dot(diag_first, link)
-    diag_second = (
-        diag_inverse[1] + gram(2) - dot(cross, link, 0, 0) - dot(link, cross_second, 0, 0)
+    whole = message[:, :, :640].reshape(512, 640)
+    diag_first, cross_second, diag_second = close(
+        core_list, whole, swap_core(whole), diag_inverse, link
     )
     return (y_first, diag_first, y_second, cross_second, diag_second, gauge.reshape(1, 1, 512))
 

time: 193 us -> 176 us (0.912)
  blocking collectives: 64.7 us -> 23.2 us
  waiting for transfers between devices: 21.6 us -> 35.5 us
  Pallas kernels: 43.9 us -> 50.1 us
  starting transfers between devices: 31.7 us -> 36.7 us
  matrix products: 5.09 us -> 0.89 us
  local copies, waits for them, and re-layouts: 5.86 us -> 9.69 us
    all_gather x1 -> x0, blocking collectives: 29 us -> none  [local(): lax.all_gather(weights, COL, axis=0, tiled=True).reshape(32, 8, 512)[:, 0]]
    all_to_all x1 -> x2, waiting for transfers between devices: 0.01 us -> 16.7 us  [the longest x1 16.2 us: local(): part = lax.all_to_all(part, plane, 0, 0, tiled=True).sum(0)]
    all_to_all x1, blocking collectives: 35.7 us -> 23.2 us  [local(): message = lax.all_to_all(message, plane, 0, 0, tiled=True)]
    pallas_call x1 -> x2, Pallas kernels: 7.36 us -> 13.8 us  [the longest x1 7.43 us: grams_of(): pl.pallas_call(gram_kernel, grid_spec=pltpu.PrefetchScalarGridSpec(num_sc...]
    dot_general x6 -> x3, matrix products: 5.09 us -> 0.89 us  [dot(): lax.dot_general(left, right, (((left_dim,), (right_dim,)), ((), ())), pre...]
    ppermute x5, starting transfers between devices: 5.59 us -> 9.74 us  [swap_core(): return lax.ppermute(value, 'core', [(0, 1), (1, 0)])]
    all_to_all x1 -> x2, starting transfers between devices: 10 us -> 11.4 us  [the longest x1 7.43 us: local(): part = lax.all_to_all(part, plane, 0, 0, tiled=True).sum(0)]
  transfers between devices with their start and end apart: 17 -> 19, of which waited for: 8 -> 9; matrix products, arithmetic and copies ran while one was open for 4% -> 6% of each run, Pallas kernels for 19% -> 25%
where the time goes in v3:
time: 176 us; the launch traced here: 175 us
  Pallas kernels  50.1 us (28%)
  starting transfers between devices  36.7 us (21%)
  waiting for transfers between devices  35.5 us (20%)
  blocking collectives  23.2 us (13%)
  between operations  14.3 us (8%)
  local copies, waits for them, and re-layouts  9.69 us (6%)
  other arithmetic  4.84 us (3%)
    pallas_call x4, Pallas kernels, add_product(): pl.pallas_call(functools.partial(product_kernel, len(pieces), has_total),...  36.3 us
    all_to_all x1, blocking collectives, local(): message = lax.all_to_all(message, plane, 0, 0, tiled=True)  23.2 us
    all_to_all x1, waiting for transfers between devices, local(): part = lax.all_to_all(part, plane, 0, 0, tiled=True).sum(0)  16.2 us
    ppermute x9, starting transfers between devices, hop(): return lax.ppermute(value, COL, pairs)  15.4 us
    ppermute x9, waiting for transfers between devices, hop(): return lax.ppermute(value, COL, pairs)  13.3 us
    ppermute x5, starting transfers between devices, swap_core(): return lax.ppermute(value, 'core', [(0, 1), (1, 0)])  9.74 us
    pallas_call x1, Pallas kernels, grams_of(): pl.pallas_call(gram_kernel, grid_spec=pltpu.PrefetchScalarGridSpec(num_sc...  7.43 us
    all_to_all x1, starting transfers between devices, local(): part = lax.all_to_all(part, plane, 0, 0, tiled=True).sum(0)  7.43 us
  transfers between devices with their start and end apart: 19, of which 9 were waited for; matrix products, arithmetic and copies ran while one was open for 6% of the time, Pallas kernels for 25%

profile of v3, /device:TPU:1, one launch (start us, length us, event | category | flops | bytes accessed | tf_op | source)
XLA Modules:
  0.0 175.3 jit_solution(16620836619597205518)
XLA Ops:
  9.0 1.5 collective-permute-start
  14.0 1.4 collective-permute-start.5
  15.4 1.4 collective-permute-start.2
  16.8 1.6 collective-permute-start.3
  18.5 5.4 %collective-permute-done.5 = f32[256,512]{1,0:T(8,128)S(1)} collective-permute-done((f32[256,512]{1,0:T(8,128)}, f32[256,512]{1,0:T(8,128)S(1)}, u32[]{:S(2)}, u32[]{:S(2)}) %collective-permute-start.5) | collective-permute-done | bytes 524320 | tf_op jit(solution)/shard_map/ppermute | solution.py:42
  24.6 1.4 collective-permute-start.6
  26.0 2.6 %collective-permute-start.7 = (f32[512,512]{1,0:T(8,128)S(1)}, f32[512,512]{1,0:T(8,128)}, u32[]{:S(2)}, u32[]{:S(2)}) collective-permute-start(f32[512,512]{1,0:T(8,128)S(1)} %pad_maximum_fusion.refs_0_), channel_id=1, source_target_pairs={{0,24},{1,7},{2,26},{3,1},{4,28},{5,3},{6,30},{7,5},{8,0},{9,15},{... | collective-permute-start | bytes 3145736 | tf_op jit(solution)/shard_map/ppermute | solution.py:42
  31.9 4.1 %collective-permute-start.4 = (f32[512,512]{1,0:T(8,128)S(1)}, f32[512,512]{1,0:T(8,128)}, u32[]{:S(2)}, u32[]{:S(2)}) collective-permute-start(f32[512,512]{1,0:T(8,128)S(1)} %constant_dynamic-update-slice_fusion.refs_1_), channel_id=1, source_target_pairs={{0,24},{1,7},{2,26},{3,1},{4,28},{5,3},{6,30},{7,5},{8,0},{9,15},{... | collective-permute-start | bytes 3145736 | tf_op jit(solution)/shard_map/ppermute | solution.py:42
  36.8 8.6 %shard_map.127.refs_2_ = f32[1024,512]{1,0:T(8,128)} custom-call(s32[5]{0:T(128)} %stack.79.order, f32[512,4096]{1,0:T(8,128)} %mine.3, f32[512,4096]{1,0:T(8,128)} %collective-permute-done.1.other, f32[512,512]{1,0:T(8,128)} %copy-done, f32[512,512]{1,0:T(8,128)} %copy-done.1), custom_call_target="tpu_custom_call" | custom-call | flops 3221225472 | bytes 5242880 | tf_op jit(solution)/shard_map/pallas_call | solution.py:84
  46.4 9.2 %shard_map.128.refs_3_ = f32[1024,512]{1,0:T(8,128)} custom-call(s32[5]{0:T(128)} %stack.74.order, f32[512,4096]{1,0:T(8,128)} %mine.3, f32[512,4096]{1,0:T(8,128)} %collective-permute-done.1.other, f32[512,512]{1,0:T(8,128)} %copy-done.4, f32[512,512]{1,0:T(8,128)} %collective-permute-done.7.refs_1_, f32[1024,512]{1,0:T(8,128)} %shard_map.127.refs_2_), custom_call_target="tpu_custom_call" | custom-call | flops 3221225472 | bytes 5242880 | tf_op jit(solution)/shard_map/pallas_call | solution.py:84
  55.7 2.7 %collective-permute-start.8 = (f32[512,512]{1,0:T(8,128)}, f32[512,512]{1,0:T(8,128)S(1)}, u32[]{:S(2)}, u32[]{:S(2)}) collective-permute-start(f32[512,512]{1,0:T(8,128)} %collective-permute-done.4.refs_1_), channel_id=1, source_target_pairs={{0,24},{1,7},{2,26},{3,1},{4,28},{5,3},{6,30},{7,5},{8,0},{9,15},{... | collective-permute-start | bytes 3145736 | tf_op jit(solution)/shard_map/ppermute | solution.py:42
  59.5 6.8 %collective-permute-done.10.refs_2_ = f32[512,512]{1,0:T(8,128)} collective-permute-done((f32[512,512]{1,0:T(8,128)S(1)}, f32[512,512]{1,0:T(8,128)}, u32[]{:S(2)}, u32[]{:S(2)}) %collective-permute-start.10) | collective-permute-done | bytes 1048608 | tf_op jit(solution)/shard_map/ppermute | solution.py:42
  66.3 11.9 %shard_map.129.refs_1_ = f32[1024,512]{1,0:T(8,128)} custom-call(s32[7]{0:T(128)} %stack.86.order, f32[512,4096]{1,0:T(8,128)} %mine.3, f32[512,4096]{1,0:T(8,128)} %collective-permute-done.1.other, f32[512,512]{1,0:T(8,128)} %collective-permute-done.9.refs_0_, f32[512,512]{1,0:T(8,128)} %collective-permute-done.4.refs_1_, ...), custom_call_target="tpu_custom_call" | custom-call | flops 4831838208 | bytes 7864320 | tf_op jit(solution)/shard_map/pallas_call | solution.py:84
  79.2 6.5 %shard_map.130.z = f32[1024,512]{1,0:T(8,128)} custom-call(s32[3]{0:T(128)} %pad_add_fusion.order, f32[512,4096]{1,0:T(8,128)} %mine.3, f32[512,4096]{1,0:T(8,128)} %collective-permute-done.1.other, f32[512,512]{1,0:T(8,128)} %copy-done.5, f32[1024,512]{1,0:T(8,128)} %shard_map.129.refs_1_), custom_call_target="tpu_custom_call" | custom-call | flops 1610612736 | bytes 2621440 | tf_op jit(solution)/shard_map/pallas_call | solution.py:84
  85.8 7.4 %shard_map.131 = f32[512,640]{1,0:T(8,128)} custom-call(s32[1]{0:T(128)} %bitcast.2.core, f32[1024,1024]{1,0:T(8,128)} %all-gather.3.cloned.1.call-done.rows, f32[1024,512]{1,0:T(8,128)} %shard_map.130.z), custom_call_target="tpu_custom_call" | custom-call | flops 2013265920 | bytes 7340032 | tf_op jit(solution)/shard_map/pallas_call | solution.py:136
  93.2 7.4 %all-to-all-start = ((f32[16,32,640]{2,1,0:T(8,128)}), f32[16,32,640]{2,1,0:T(8,128)S(1)}, u32[]{:S(2)}, u32[]{:S(2)}) async-start(f32[16,32,640]{2,1,0:T(8,128)} %bitcast.65), calls=%async_computation.1 | async-start | bytes 2621440 | tf_op jit(solution)/shard_map/all_to_all | solution.py:280
  102.0 16.2 %all-to-all-done = f32[16,32,640]{2,1,0:T(8,128)S(1)} async-done(((f32[16,32,640]{2,1,0:T(8,128)}), f32[16,32,640]{2,1,0:T(8,128)S(1)}, u32[]{:S(2)}, u32[]{:S(2)}) %all-to-all-start) | async-done | bytes 1310752 | tf_op jit(solution)/shard_map/all_to_all | solution.py:280
  119.0 4.0 %all-to-all-start.1 = ((f32[4,32,640]{2,1,0:T(8,128)}), f32[4,32,640]{2,1,0:T(8,128)S(1)}, u32[]{:S(2)}, u32[]{:S(2)}) async-start(f32[4,32,640]{2,1,0:T(8,128)} %broadcast_in_dim.10), calls=%async_computation.2 | async-start | bytes 655360 | tf_op jit(solution)/shard_map/all_to_all | solution.py:282
  123.0 1.4 reduce-scatter.2.cloned.1.call-done
  125.6 2.7 %collective-permute-start.11 = (f32[128,512]{1,0:T(8,128)S(1)}, f32[128,512]{1,0:T(8,128)S(1)}, u32[]{:S(2)}, u32[]{:S(2)}) collective-permute-start(f32[128,512]{1,0:T(8,128)S(1)} %slice_select_fusion), channel_id=1, source_target_pairs={{0,1},{1,0},{2,3},{3,2},{4,5},{5,4},{6,7},{7,6},{8,9},{9,8},{10,11... | collective-permute-start | bytes 786440 | tf_op jit(solution)/shard_map/ppermute | solution.py:31
  130.8 23.2 %all_to_all.15 = f32[16,32,768]{2,1,0:T(8,128)S(1)} all-to-all(f32[16,32,768]{2,1,0:T(8,128)S(1)} %select_maximum_fusion), channel_id=1, replica_groups=mesh['x'=4,'y'=4,'z'=4,'core'=2] {'y','z'}, dimensions={0} | all-to-all | bytes 3145728 | tf_op jit(solution)/shard_map/all_to_all | solution.py:293
  154.2 5.1 %collective-permute-start.12 = (f32[512,640]{1,0:T(8,128)S(1)}, f32[512,640]{1,0:T(8,128)}, u32[]{:S(2)}, u32[]{:S(2)}) collective-permute-start(f32[512,640]{1,0:T(8,128)S(1)} %bitcast.67), channel_id=1, source_target_pairs={{0,1},{1,0},{2,3},{3,2},{4,5},{5,4},{6,7},{7,6},{8,9},{9,8},{10,11... | collective-permute-start | bytes 3932168 | tf_op jit(solution)/shard_map/ppermute | solution.py:31
  159.4 2.4 %collective-permute-done.13 = f32[1,512]{1,0:T(1,128)S(1)} collective-permute-done((f32[1,512]{1,0:T(1,128)S(1)}, f32[1,512]{1,0:T(1,128)S(1)}, u32[]{:S(2)}, u32[]{:S(2)}) %collective-permute-start.13) | collective-permute-done | bytes 2080 | tf_op jit(solution)/shard_map/ppermute | solution.py:31
  162.4 6.4 %shard_map.132 = (f32[512,512]{1,0:T(8,128)}, f32[512,512]{1,0:T(8,128)}, f32[512,512]{1,0:T(8,128)}) custom-call(s32[1]{0:T(128)} %bitcast.2.core, f32[512,640]{1,0:T(8,128)} %bitcast.68, f32[512,640]{1,0:T(8,128)} %collective-permute-done.12.theirs, f32[2,512,512]{2,1,0:T(8,128)} %diag.1, f32[512,512]{1,0:T(8,128)} %link.1), custom_call_target="tpu_custom_call" | custom-call | flops 4831838208 | bytes 9437184 | tf_op jit(solution)/shard_map/pallas_call | solution.py:192
  (89 shorter events, 19.3 us)
Async XLA Ops:
  7.2 71.1 %all-gather.3.cloned.1.call-start = ((), (), s32[]{:S(2)}) async-start(), calls=%async_computation.4 | async-start | bytes 4718592 | tf_op jit(solution)/shard_map/all_gather | solution.py:235
  9.0 2.7 %collective-permute-start = (f32[2,128,256]{2,1,0:T(8,128)S(1)}, f32[2,128,256]{2,1,0:T(8,128)S(1)}, u32[]{:S(2)}, u32[]{:S(2)}) collective-permute-start(f32[2,128,256]{2,1,0:T(8,128)S(1)} %fusion.4), channel_id=1, source_target_pairs={{0,1},{1,0},{2,3},{3,2},{4,5},{5,4},{6,7},{7,6},{8,9},{9,8},{10,11... | collective-permute-start | bytes 786440 | tf_op jit(solution)/shard_map/ppermute | solution.py:31
  11.7 25.1 %collective-permute-start.1 = (f32[512,4096]{1,0:T(8,128)}, f32[512,4096]{1,0:T(8,128)}, u32[]{:S(2)}, u32[]{:S(2)}) collective-permute-start(f32[512,4096]{1,0:T(8,128)} %mine.3), channel_id=1, source_target_pairs={{0,1},{1,0},{2,3},{3,2},{4,5},{5,4},{6,7},{7,6},{8,9},{9,8},{10,11... | collective-permute-start | bytes 25165832 | tf_op jit(solution)/shard_map/ppermute | solution.py:31
  13.0 10.9 %copy-start.9 = (f32[1,1,512]{2,1,0:T(1,128)S(1)}, f32[1,1,512]{2,1,0:T(1,128)}, u32[]{:S(2)}) copy-start(f32[1,1,512]{2,1,0:T(1,128)} %param.15) | copy-start | bytes 6148
  13.0 87.9 %all-gather.5.cloned.1.call-start = ((), (), s32[]{:S(2)}) async-start(), calls=%async_computation.6 | async-start | bytes 1081344 | tf_op jit(solution)/shard_map/all_gather | solution.py:242
  14.0 9.9 %collective-permute-start.5 = (f32[256,512]{1,0:T(8,128)}, f32[256,512]{1,0:T(8,128)S(1)}, u32[]{:S(2)}, u32[]{:S(2)}) collective-permute-start(f32[256,512]{1,0:T(8,128)} %pad_maximum_fusion.1), channel_id=1, source_target_pairs={{0,2},{1,9},{2,4},{3,11},{4,6},{5,13},{6,0},{7,15},{8,10},{9,17},{... | collective-permute-start | bytes 1572872 | tf_op jit(solution)/shard_map/ppermute | solution.py:42
  15.4 13.3 %collective-permute-start.2 = (f32[256,512]{1,0:T(8,128)}, f32[256,512]{1,0:T(8,128)}, u32[]{:S(2)}, u32[]{:S(2)}) collective-permute-start(f32[256,512]{1,0:T(8,128)} %pad_maximum_fusion.1), channel_id=1, source_target_pairs={{0,6},{1,25},{2,0},{3,27},{4,2},{5,29},{6,4},{7,31},{8,14},{9,1},{... | collective-permute-start | bytes 1572872 | tf_op jit(solution)/shard_map/ppermute | solution.py:42
  16.8 14.0 %collective-permute-start.3 = (f32[256,512]{1,0:T(8,128)}, f32[256,512]{1,0:T(8,128)}, u32[]{:S(2)}, u32[]{:S(2)}) collective-permute-start(f32[256,512]{1,0:T(8,128)} %pad_maximum_fusion.1), channel_id=1, source_target_pairs={{0,4},{1,17},{2,6},{3,19},{4,0},{5,21},{6,2},{7,23},{8,12},{9,25},... | collective-permute-start | bytes 1572872 | tf_op jit(solution)/shard_map/ppermute | solution.py:42
  24.6 12.2 %copy-start = (f32[512,512]{1,0:T(8,128)}, f32[512,512]{1,0:T(8,128)S(1)}, u32[]{:S(2)}) copy-start(f32[512,512]{1,0:T(8,128)S(1)} %pad_maximum_fusion.refs_0_) | copy-start | bytes 3145732
  24.6 20.8 %collective-permute-start.6 = (f32[512,512]{1,0:T(8,128)S(1)}, f32[512,512]{1,0:T(8,128)S(1)}, u32[]{:S(2)}, u32[]{:S(2)}) collective-permute-start(f32[512,512]{1,0:T(8,128)S(1)} %pad_maximum_fusion.refs_0_), channel_id=1, source_target_pairs={{0,8},{1,3},{2,10},{3,5},{4,12},{5,7},{6,14},{7,1},{8,16},{9,11},{... | collective-permute-start | bytes 3145736 | tf_op jit(solution)/shard_map/ppermute | solution.py:42
  26.0 20.3 %collective-permute-start.7 = (f32[512,512]{1,0:T(8,128)S(1)}, f32[512,512]{1,0:T(8,128)}, u32[]{:S(2)}, u32[]{:S(2)}) collective-permute-start(f32[512,512]{1,0:T(8,128)S(1)} %pad_maximum_fusion.refs_0_), channel_id=1, source_target_pairs={{0,24},{1,7},{2,26},{3,1},{4,28},{5,3},{6,30},{7,5},{8,0},{9,15},{... | collective-permute-start | bytes 3145736 | tf_op jit(solution)/shard_map/ppermute | solution.py:42
  31.9 23.8 %collective-permute-start.4 = (f32[512,512]{1,0:T(8,128)S(1)}, f32[512,512]{1,0:T(8,128)}, u32[]{:S(2)}, u32[]{:S(2)}) collective-permute-start(f32[512,512]{1,0:T(8,128)S(1)} %constant_dynamic-update-slice_fusion.refs_1_), channel_id=1, source_target_pairs={{0,24},{1,7},{2,26},{3,1},{4,28},{5,3},{6,30},{7,5},{8,0},{9,15},{... | collective-permute-start | bytes 3145736 | tf_op jit(solution)/shard_map/ppermute | solution.py:42
  36.1 88.4 %reduce-scatter.2.cloned.1.call-start = ((), (), s32[]{:S(2)}) async-start(), calls=%async_computation.5 | async-start | bytes 2621440 | tf_op jit(solution)/shard_map/reduce_scatter | solution.py:278
  36.8 22.7 %collective-permute-start.9 = (f32[512,512]{1,0:T(8,128)S(1)}, f32[512,512]{1,0:T(8,128)}, u32[]{:S(2)}, u32[]{:S(2)}) collective-permute-start(f32[512,512]{1,0:T(8,128)S(1)} %constant_dynamic-update-slice_fusion.refs_1_), channel_id=1, source_target_pairs={{0,8},{1,3},{2,10},{3,5},{4,12},{5,7},{6,14},{7,1},{8,16},{9,11},{... | collective-permute-start | bytes 3145736 | tf_op jit(solution)/shard_map/ppermute | solution.py:42
  45.5 20.8 %collective-permute-start.10 = (f32[512,512]{1,0:T(8,128)S(1)}, f32[512,512]{1,0:T(8,128)}, u32[]{:S(2)}, u32[]{:S(2)}) collective-permute-start(f32[512,512]{1,0:T(8,128)S(1)} %collective-permute-done.6.refs_0_), channel_id=1, source_target_pairs={{0,8},{1,3},{2,10},{3,5},{4,12},{5,7},{6,14},{7,1},{8,16},{9,11},{... | collective-permute-start | bytes 3145736 | tf_op jit(solution)/shard_map/ppermute | solution.py:42
  55.7 22.6 %collective-permute-start.8 = (f32[512,512]{1,0:T(8,128)}, f32[512,512]{1,0:T(8,128)S(1)}, u32[]{:S(2)}, u32[]{:S(2)}) collective-permute-start(f32[512,512]{1,0:T(8,128)} %collective-permute-done.4.refs_1_), channel_id=1, source_target_pairs={{0,24},{1,7},{2,26},{3,1},{4,28},{5,3},{6,30},{7,5},{8,0},{9,15},{... | collective-permute-start | bytes 3145736 | tf_op jit(solution)/shard_map/ppermute | solution.py:42
  93.2 7.4 %copy-start.11 = (s32[1,1,32]{2,1,0:T(1,128)S(1)}, s32[1,1,32]{2,1,0:T(1,128)}, u32[]{:S(2)}) copy-start(s32[1,1,32]{2,1,0:T(1,128)} %param.13) | copy-start | bytes 388
  93.2 7.4 %copy-start.12 = (s32[1,1,32]{2,1,0:T(1,128)S(1)}, s32[1,1,32]{2,1,0:T(1,128)}, u32[]{:S(2)}) copy-start(s32[1,1,32]{2,1,0:T(1,128)} %param.14) | copy-start | bytes 388
  93.2 25.0 %all-to-all-start = ((f32[16,32,640]{2,1,0:T(8,128)}), f32[16,32,640]{2,1,0:T(8,128)S(1)}, u32[]{:S(2)}, u32[]{:S(2)}) async-start(f32[16,32,640]{2,1,0:T(8,128)} %bitcast.65), calls=%async_computation.1 | async-start | bytes 2621440 | tf_op jit(solution)/shard_map/all_to_all | solution.py:280
  119.0 9.9 %all-to-all-start.1 = ((f32[4,32,640]{2,1,0:T(8,128)}), f32[4,32,640]{2,1,0:T(8,128)S(1)}, u32[]{:S(2)}, u32[]{:S(2)}) async-start(f32[4,32,640]{2,1,0:T(8,128)} %broadcast_in_dim.10), calls=%async_computation.2 | async-start | bytes 655360 | tf_op jit(solution)/shard_map/all_to_all | solution.py:282
  125.6 3.8 %collective-permute-start.11 = (f32[128,512]{1,0:T(8,128)S(1)}, f32[128,512]{1,0:T(8,128)S(1)}, u32[]{:S(2)}, u32[]{:S(2)}) collective-permute-start(f32[128,512]{1,0:T(8,128)S(1)} %slice_select_fusion), channel_id=1, source_target_pairs={{0,1},{1,0},{2,3},{3,2},{4,5},{5,4},{6,7},{7,6},{8,9},{9,8},{10,11... | collective-permute-start | bytes 786440 | tf_op jit(solution)/shard_map/ppermute | solution.py:31
  154.2 8.2 %copy-start.3 = (f32[16,32,640]{2,1,0:T(8,128)}, f32[16,32,640]{2,1,0:T(8,128)S(1)}, u32[]{:S(2)}) copy-start(f32[16,32,640]{2,1,0:T(8,128)S(1)} %slice.105) | copy-start | bytes 3932164
  154.2 8.2 %collective-permute-start.12 = (f32[512,640]{1,0:T(8,128)S(1)}, f32[512,640]{1,0:T(8,128)}, u32[]{:S(2)}, u32[]{:S(2)}) collective-permute-start(f32[512,640]{1,0:T(8,128)S(1)} %bitcast.67), channel_id=1, source_target_pairs={{0,1},{1,0},{2,3},{3,2},{4,5},{5,4},{6,7},{7,6},{8,9},{9,8},{10,11... | collective-permute-start | bytes 3932168 | tf_op jit(solution)/shard_map/ppermute | solution.py:31
  159.3 2.5 %collective-permute-start.13 = (f32[1,512]{1,0:T(1,128)S(1)}, f32[1,512]{1,0:T(1,128)S(1)}, u32[]{:S(2)}, u32[]{:S(2)}) collective-permute-start(f32[1,512]{1,0:T(1,128)S(1)} %bitcast.74), channel_id=1, source_target_pairs={{0,1},{1,0},{2,3},{3,2},{4,5},{5,4},{6,7},{7,6},{8,9},{9,8},{10,11... | collective-permute-start | bytes 6152 | tf_op jit(solution)/shard_map/ppermute | solution.py:31
  (8 other events, 16.2 us)
Sparse Core Ops, SparseCore 0:
  13.1 34.4 all-gather.2
  50.4 43.1 all-gather.4
  96.0 28.4 reduce-scatter.1

commit v4 on v3

--- a/solution.py
+++ b/solution.py
@@ -47,60 +47,85 @@
     return high, (value - high.astype(F32)).astype(BF16)
 
 
-def product_kernel(count, has_total, order, mine, other, *refs):
-    pieces = refs[:count]
-    out, piece_high, piece_low = refs[-3:]
+def product_kernel(count, has_total, has_gram, order, *refs):
+    blocks, refs = refs[:4], refs[4:]
+    pieces, refs = refs[:count], refs[count:]
+    total, refs = (refs[0], refs[1:]) if has_total else (None, refs)
+    rows, refs = (refs[0], refs[1:]) if has_gram else (None, refs)
+    out, piece_high, piece_low = refs[0], refs[-2], refs[-1]
     step = pl.program_id(0)
-    core = order[pl.num_programs(0)]
+    core = order[2 * pl.num_programs(0)]
 
     @pl.when(step == 0)
     def _():
         at = 0
         for piece in pieces:
-            rows = piece.shape[0]
-            piece_high[at : at + rows, :], piece_low[at : at + rows, :] = parts(piece[...])
-            at += rows
-        out[...] = refs[count][...] if has_total else jnp.zeros_like(out)
-
-    at = pl.ds(pl.multiple_of(step * 256, 256), 256)
+            count_rows = piece.shape[0]
+            to = slice(at, at + count_rows)
+            piece_high[to, :], piece_low[to, :] = parts(piece[...])
+            at += count_rows
+        out[...] = total[...] if has_total else jnp.zeros_like(out)
+
+    at = pl.ds(pl.multiple_of(step * 512, 512), 512)
     high, low = piece_high[at, :], piece_low[at, :]
     right = jnp.concatenate([high, low, high], axis=0)
-    for source, side in ((mine, core), (other, 1 - core)):
-        top, rest = parts(source[...])
-        left = jnp.concatenate([top, top, rest], axis=1)
+    for one, two, side in ((blocks[0], blocks[1], core), (blocks[2], blocks[3], 1 - core)):
+        one, two = parts(one[...]), parts(two[...])
+        left = jnp.concatenate([one[0], two[0], one[0], two[0], one[1], two[1]], axis=1)
         made = jnp.dot(left, right, preferred_element_type=F32)
         for row in range(4):
             to = pl.ds(pl.multiple_of(row * 256 + side * 128, 128), 128)
             out[to, :] += made[row * 128 : row * 128 + 128, :]
 
-
-def add_product(order, mine, other, pieces, total=None):
+    if has_gram:
+
+        @pl.when(step == pl.num_programs(0) - 1)
+        def _():
+            gram_of(core == 0, rows, out, refs[1])
+
+
+def add_product(order, mine, other, pieces, total=None, rows=None):
     depth = sum(piece.shape[0] for piece in pieces)
-    block = pl.BlockSpec((512, 256), lambda j, order: (0, order[j]))
-    whole = [pl.BlockSpec(piece.shape, lambda j, order: (0, 0)) for piece in pieces]
-    made = pl.BlockSpec((1024, 512), lambda j, order: (0, 0))
-    has_total = total is not None
-    args = [order, mine, other, *pieces] + ([total] if has_total else [])
-    return pl.pallas_call(
-        functools.partial(product_kernel, len(pieces), has_total),
+    one = pl.BlockSpec((512, 256), lambda j, order: (0, order[2 * j]))
+    two = pl.BlockSpec((512, 256), lambda j, order: (0, order[2 * j + 1]))
+
+    def fixed(shape):
+        return pl.BlockSpec(shape, lambda j, order: (0, 0))
+
+    made = fixed((1024, 512))
+    has_total, has_gram = total is not None, rows is not None
+    args = [order, mine, mine, other, other, *pieces]
+    in_specs = [one, two, one, two] + [fixed(piece.shape) for piece in pieces]
+    out_specs, out_shape = [made], [jax.ShapeDtypeStruct((1024, 512), F32)]
+    if has_total:
+        args.append(total)
+        in_specs.append(made)
+    if has_gram:
+        args.append(rows)
+        in_specs.append(fixed((1024, 1024)))
+        out_specs.append(fixed((512, 640)))
+        out_shape.append(jax.ShapeDtypeStruct((512, 640), F32))
+    made = pl.pallas_call(
+        functools.partial(product_kernel, len(pieces), has_total, has_gram),
         grid_spec=pltpu.PrefetchScalarGridSpec(
             num_scalar_prefetch=1,
-            grid=(depth // 256,),
-            in_specs=[block, block, *whole] + ([made] if has_total else []),
-            out_specs=made,
+            grid=(depth // 512,),
+            in_specs=in_specs,
+            out_specs=out_specs,
             scratch_shapes=[pltpu.VMEM((depth, 512), BF16)] * 2,
         ),
-        out_shape=jax.ShapeDtypeStruct((1024, 512), F32),
+        out_shape=out_shape,
         cost_estimate=pl.CostEstimate(
             flops=6 * 1024 * 512 * depth, bytes_accessed=5120 * depth, transcendentals=0
         ),
+        compiler_params=pltpu.CompilerParams(vmem_limit_bytes=48 << 20),
     )(*args)
-
-
-def gram_kernel(core, rows, z, out):
+    return made if has_gram else made[0]
+
+
+def gram_of(first, rows, z, out):
     rows_high, rows_low = parts(rows[...])
     z_high, z_low = parts(z[...])
-    first = core[0] == 0
 
     def product(left, right):
         def terms(one, two):
@@ -117,38 +142,15 @@
     def either(one, two):
         return tuple(jnp.where(first, left, right) for left, right in zip(one, two))
 
-    @pl.when(pl.program_id(0) == 0)
-    def _():
-        out[...] = jnp.zeros_like(out)
-
-    out[:, :256] += product(panel(0, 512), kept(256, 512))
+    out[:, :256] = product(panel(0, 512), kept(256, 512))
     for slot in range(2):
         at, start, half = slice(slot * 256, slot * 256 + 256), slot * 512, slot * 256
         low, high = panel(start, start + 256), panel(start + 256, start + 512)
         mine = kept(half, half + 256)
-        out[at, 256:512] += product(either(low, high), mine)
-        out[at, 512:] += product(
+        out[at, 256:512] = product(either(low, high), mine)
+        out[at, 512:] = product(
             either(high, mine), either(kept(half, half + 128), panel(start + 128, start + 256))
         )
-
-
-def grams_of(core, rows, z):
-    return pl.pallas_call(
-        gram_kernel,
-        grid_spec=pltpu.PrefetchScalarGridSpec(
-            num_scalar_prefetch=1,
-            grid=(4,),
-            in_specs=[
-                pl.BlockSpec((256, 1024), lambda k, core: (k, 0)),
-                pl.BlockSpec((256, 512), lambda k, core: (k, 0)),
-            ],
-            out_specs=pl.BlockSpec((512, 640), lambda k, core: (0, 0)),
-        ),
-        out_shape=jax.ShapeDtypeStruct((512, 640), F32),
-        cost_estimate=pl.CostEstimate(
-            flops=6 * 1024 * 512 * 640, bytes_accessed=7 << 20, transcendentals=0
-        ),
-    )(core, rows, z)
 
 
 def close_kernel(core, mine, theirs, diag, link, diag_first, cross_second, diag_second):
@@ -237,10 +239,6 @@
     behind = hop(own, 0, 1)
     ahead = hop(own, 0, -1)
     across = hop(own, 0, 2)
-    weights = jnp.broadcast_to(gauge_weight.reshape(1, 512), (16, 512))
-    weights, behind = lax.optimization_barrier((weights, behind))
-    weights = lax.all_gather(weights, COL, axis=0, tiled=True).reshape(32, 16, 512)[:, 0]
-    weights = lax.dynamic_slice_in_dim(weights, col * IBR, IBR, axis=1)
     pair = jnp.concatenate([own, behind], axis=0)
     pair_behind = hop(pair, 1, 1)
     pair_ahead = hop(pair, 1, -1)
@@ -253,8 +251,10 @@
     z = add_product(
         order_of((0, -1), (-1, -1), (0, 1), (-1, 1)), ancestor, other, (pair_behind, pair_ahead), z
     )
-    rest_ahead, z = lax.optimization_barrier((rest_ahead, z))
+    weights = gauge_weight.reshape(32, IBR)
+    rest_ahead, z, weights = lax.optimization_barrier((rest_ahead, z, weights))
     rest_across = hop(rest_ahead, 1, -1)
+    weights = lax.all_to_all(weights, COL, 0, 0, tiled=True)
     z = add_product(
         order_of((1, -1), (2, -1), (1, 1), (2, 1), (0, 2), (-1, 2)),
         ancestor,
@@ -262,8 +262,10 @@
         (rest_behind, rest_ahead, pair_across),
         z,
     )
-    z, rows = lax.optimization_barrier((z, rows))
-    z = add_product(order_of((1, 2), (2, 2)), ancestor, other, (rest_across,), z)
+    z, rows, weights = lax.optimization_barrier((z, rows, weights))
+    z, part = add_product(
+        order_of((1, 2), (2, 2)), ancestor, other, (rest_across,), z, rows
+    )
 
     owner_match = (
         gauge_owner[0, 0][None, :] == jnp.arange(32, dtype=jnp.int32)[:, None]
@@ -276,8 +278,7 @@
     core_list = core.astype(jnp.int32).reshape(1)
     plane = ("y", "z")
     z_pair = lax.psum_scatter(z, "x", scatter_dimension=0, tiled=True)
-    part = grams_of(core_list, rows, z).reshape(16, 32, 640)
-    part = lax.all_to_all(part, plane, 0, 0, tiled=True).sum(0)
+    part = lax.all_to_all(part.reshape(16, 32, 640), plane, 0, 0, tiled=True).sum(0)
     part = jnp.broadcast_to(part[None], (4, 32, 640))
     part = lax.all_to_all(part, "x", 0, 0, tiled=True).sum(0)
 

time: 176 us -> 172 us (0.977)
  blocking collectives: 23.2 us -> 52.3 us
  waiting for transfers between devices: 35.5 us -> 16.6 us
  Pallas kernels: 50.1 us -> 38.5 us
  starting transfers between devices: 36.7 us -> 33.6 us
    all_to_all x0 -> x1, blocking collectives: none -> 23.6 us  [local(): lax.all_to_all(part.reshape(16, 32, 640), plane, 0, 0, tiled=True).sum(0)]
    all_to_all x1, waiting for transfers between devices: 16.2 us -> 0.01 us  [local(): weights = lax.all_to_all(weights, COL, 0, 0, tiled=True)]
    pallas_call x5 -> x4, Pallas kernels: 43.7 us -> 32.1 us  [add_product(): pl.pallas_call(functools.partial(product_kernel, len(pieces), has_total,...]
    all_to_all x1, blocking collectives: 23.2 us -> 28.7 us  [local(): message = lax.all_to_all(message, plane, 0, 0, tiled=True)]
    unnamed x28 -> x31, local copies, waits for them, and re-layouts: 3.69 us -> 8.6 us
    ppermute x5, starting transfers between devices: 9.74 us -> 5.02 us  [swap_core(): return lax.ppermute(value, 'core', [(0, 1), (1, 0)])]
    ppermute x9, waiting for transfers between devices: 13.3 us -> 8.64 us  [hop(): return lax.ppermute(value, COL, pairs)]
    reduce_scatter x1, waiting for transfers between devices: 1.41 us -> 3.56 us  [local(): z_pair = lax.psum_scatter(z, 'x', scatter_dimension=0, tiled=True)]
  transfers between devices with their start and end apart: 19 -> 18, of which waited for: 9 -> 10; matrix products, arithmetic and copies ran while one was open for 6% -> 4% of each run, Pallas kernels for 25% -> 14%
where the time goes in v4:
time: 172 us; the launch traced here: 171 us
  blocking collectives  52.3 us (30%)
  Pallas kernels  38.5 us (22%)
  starting transfers between devices  33.6 us (20%)
  waiting for transfers between devices  16.6 us (10%)
  between operations  14.4 us (8%)
  local copies, waits for them, and re-layouts  10.9 us (6%)
  other arithmetic  4.2 us (2%)
    pallas_call x4, Pallas kernels, add_product(): pl.pallas_call(functools.partial(product_kernel, len(pieces), has_total,...  32.1 us
    all_to_all x1, blocking collectives, local(): message = lax.all_to_all(message, plane, 0, 0, tiled=True)  28.7 us
    all_to_all x1, blocking collectives, local(): lax.all_to_all(part.reshape(16, 32, 640), plane, 0, 0, tiled=True).sum(0)  23.6 us
    ppermute x9, starting transfers between devices, hop(): return lax.ppermute(value, COL, pairs)  16 us
    ppermute x9, waiting for transfers between devices, hop(): return lax.ppermute(value, COL, pairs)  8.64 us
    unnamed x31, local copies, waits for them, and re-layouts  8.6 us
    all_to_all x1, starting transfers between devices, local(): weights = lax.all_to_all(weights, COL, 0, 0, tiled=True)  8.21 us
    pallas_call x1, Pallas kernels, close(): pl.pallas_call(close_kernel, in_specs=[pl.BlockSpec(memory_space=pltpu.SM...  6.37 us
  transfers between devices with their start and end apart: 18, of which 10 were waited for; matrix products, arithmetic and copies ran while one was open for 4% of the time, Pallas kernels for 14%

profile of v4, /device:TPU:1, one launch (start us, length us, event | category | flops | bytes accessed | tf_op | source)
XLA Modules:
  0.0 171.4 jit_solution(16060268652248554641)
XLA Ops:
  9.0 1.5 collective-permute-start
  13.1 1.4 collective-permute-start.5
  14.6 1.5 collective-permute-start.2
  16.1 1.6 collective-permute-start.3
  17.7 5.2 %collective-permute-done.5 = f32[256,512]{1,0:T(8,128)S(1)} collective-permute-done((f32[256,512]{1,0:T(8,128)S(1)}, f32[256,512]{1,0:T(8,128)S(1)}, u32[]{:S(2)}, u32[]{:S(2)}) %collective-permute-start.5) | collective-permute-done | bytes 524320 | tf_op jit(solution)/shard_map/ppermute | solution.py:42
  23.0 1.4 collective-permute-start.6
  24.4 2.5 %collective-permute-start.7 = (f32[512,512]{1,0:T(8,128)S(1)}, f32[512,512]{1,0:T(8,128)}, u32[]{:S(2)}, u32[]{:S(2)}) collective-permute-start(f32[512,512]{1,0:T(8,128)S(1)} %pad_maximum_fusion.refs_4_), channel_id=1, source_target_pairs={{0,24},{1,7},{2,26},{3,1},{4,28},{5,3},{6,30},{7,5},{8,0},{9,15},{... | collective-permute-start | bytes 3145736 | tf_op jit(solution)/shard_map/ppermute | solution.py:42
  27.9 1.8 %collective-permute-done.3 = f32[256,512]{1,0:T(8,128)S(1)} collective-permute-done((f32[256,512]{1,0:T(8,128)S(1)}, f32[256,512]{1,0:T(8,128)S(1)}, u32[]{:S(2)}, u32[]{:S(2)}) %collective-permute-start.3) | collective-permute-done | bytes 524320 | tf_op jit(solution)/shard_map/ppermute | solution.py:42
  29.7 4.9 %collective-permute-start.4 = (f32[512,512]{1,0:T(8,128)S(1)}, f32[512,512]{1,0:T(8,128)S(1)}, u32[]{:S(2)}, u32[]{:S(2)}) collective-permute-start(f32[512,512]{1,0:T(8,128)S(1)} %constant_dynamic-update-slice_fusion.refs_5_), channel_id=1, source_target_pairs={{0,24},{1,7},{2,26},{3,1},{4,28},{5,3},{6,30},{7,5},{8,0},{9,15},{... | collective-permute-start | bytes 3145736 | tf_op jit(solution)/shard_map/ppermute | solution.py:42
  34.7 6.2 %shard_map.127.refs_6_ = f32[1024,512]{1,0:T(8,128)S(1)} custom-call(s32[5]{0:T(128)S(1)} %stack.79.order, f32[512,4096]{1,0:T(8,128)} %refs_1_.3, f32[512,4096]{1,0:T(8,128)} %refs_1_.3, f32[512,4096]{1,0:T(8,128)} %collective-permute-done.1.refs_2_.refs_3_, f32[512,4096]{1,0:T(8,128)} %collective-permute-done.1.refs_2_.refs_3_, ...), custom_call_target="tpu_custom_call" | custom-call | flops 3221225472 | bytes 5242880 | tf_op jit(solution)/shard_map/pallas_call | solution.py:108
  40.9 1.3 copy-done
  44.6 7.6 %shard_map.128.refs_7_ = f32[1024,512]{1,0:T(8,128)S(1)} custom-call(s32[5]{0:T(128)S(1)} %stack.74.order, f32[512,4096]{1,0:T(8,128)} %refs_1_.3, f32[512,4096]{1,0:T(8,128)} %refs_1_.3, f32[512,4096]{1,0:T(8,128)} %collective-permute-done.1.refs_2_.refs_3_, f32[512,4096]{1,0:T(8,128)} %collective-permute-done.1.refs_2_.refs_3_, ...), custom_call_target="tpu_custom_call" | custom-call | flops 3221225472 | bytes 5242880 | tf_op jit(solution)/shard_map/pallas_call | solution.py:108
  53.5 2.7 %collective-permute-start.8 = (f32[512,512]{1,0:T(8,128)S(1)}, f32[512,512]{1,0:T(8,128)S(1)}, u32[]{:S(2)}, u32[]{:S(2)}) collective-permute-start(f32[512,512]{1,0:T(8,128)S(1)} %collective-permute-done.4.refs_5_), channel_id=1, source_target_pairs={{0,24},{1,7},{2,26},{3,1},{4,28},{5,3},{6,30},{7,5},{8,0},{9,15},{... | collective-permute-start | bytes 3145736 | tf_op jit(solution)/shard_map/ppermute | solution.py:42
  56.4 8.2 %all-to-all-start = ((f32[32,1,16]{2,1,0:T(1,128)}), f32[32,1,16]{2,1,0:T(1,128)S(1)}, u32[]{:S(2)}, u32[]{:S(2)}) async-start(f32[32,1,16]{2,1,0:T(1,128)} %bitcast.30), calls=%async_computation | async-start | bytes 32768 | tf_op jit(solution)/shard_map/all_to_all | solution.py:257
  65.1 9.6 %shard_map.129.refs_5_ = f32[1024,512]{1,0:T(8,128)S(1)} custom-call(s32[7]{0:T(128)S(1)} %stack.86.order, f32[512,4096]{1,0:T(8,128)} %refs_1_.3, f32[512,4096]{1,0:T(8,128)} %refs_1_.3, f32[512,4096]{1,0:T(8,128)} %collective-permute-done.1.refs_2_.refs_3_, f32[512,4096]{1,0:T(8,128)} %collective-permute-done.1.refs_2_.refs_3_, ...), custom_call_target="tpu_custom_call" | custom-call | flops 4831838208 | bytes 7864320 | tf_op jit(solution)/shard_map/pallas_call | solution.py:108
  74.7 1.3 copy-done.2
  78.2 8.7 %shard_map.130 = (f32[1024,512]{1,0:T(8,128)}, f32[512,640]{1,0:T(8,128)S(1)}) custom-call(s32[3]{0:T(128)S(1)} %pad_add_fusion.order, f32[512,4096]{1,0:T(8,128)} %refs_1_.3, f32[512,4096]{1,0:T(8,128)} %refs_1_.3, f32[512,4096]{1,0:T(8,128)} %collective-permute-done.1.refs_2_.refs_3_, f32[512,4096]{1,0:T(8,128)} %collective-permute-done.1.refs_2_.refs_3_, ...), custom_call_target="tpu_custom_call" | custom-call | flops 1610612736 | bytes 2621440 | tf_op jit(solution)/shard_map/pallas_call | solution.py:108
  87.0 23.6 %all_to_all.27 = f32[16,32,640]{2,1,0:T(8,128)S(1)} all-to-all(f32[16,32,640]{2,1,0:T(8,128)S(1)} %bitcast.66), channel_id=1, replica_groups=mesh['x'=4,'y'=4,'z'=4,'core'=2] {'y','z'}, dimensions={0} | all-to-all | bytes 2621440 | tf_op jit(solution)/shard_map/all_to_all | solution.py:281
  111.4 4.1 %all-to-all-start.2 = ((f32[4,32,640]{2,1,0:T(8,128)}), f32[4,32,640]{2,1,0:T(8,128)S(1)}, u32[]{:S(2)}, u32[]{:S(2)}) async-start(f32[4,32,640]{2,1,0:T(8,128)} %broadcast_in_dim.4), calls=%async_computation.3 | async-start | bytes 655360 | tf_op jit(solution)/shard_map/all_to_all | solution.py:283
  115.5 3.6 %reduce-scatter.2.cloned.1.call-done = f32[256,512]{1,0:T(8,128)} async-done(((f32[1024,512]{1,0:T(8,128)}), f32[256,512]{1,0:T(8,128)}) %reduce-scatter.2.cloned.1.call-update) | async-done | bytes 524304 | tf_op jit(solution)/shard_map/reduce_scatter | solution.py:280
  123.9 28.7 %all_to_all.28 = f32[16,32,768]{2,1,0:T(8,128)S(1)} all-to-all(f32[16,32,768]{2,1,0:T(8,128)S(1)} %select_maximum_fusion), channel_id=1, replica_groups=mesh['x'=4,'y'=4,'z'=4,'core'=2] {'y','z'}, dimensions={0} | all-to-all | bytes 3145728 | tf_op jit(solution)/shard_map/all_to_all | solution.py:294
  152.7 2.4 %collective-permute-start.12 = (f32[512,640]{1,0:T(8,128)S(1)}, f32[512,640]{1,0:T(8,128)}, u32[]{:S(2)}, u32[]{:S(2)}) collective-permute-start(f32[512,640]{1,0:T(8,128)S(1)} %bitcast.68), channel_id=1, source_target_pairs={{0,1},{1,0},{2,3},{3,2},{4,5},{5,4},{6,7},{7,6},{8,9},{9,8},{10,11... | collective-permute-start | bytes 3932168 | tf_op jit(solution)/shard_map/ppermute | solution.py:31
  155.2 2.4 %collective-permute-done.13 = f32[1,512]{1,0:T(1,128)S(1)} collective-permute-done((f32[1,512]{1,0:T(1,128)S(1)}, f32[1,512]{1,0:T(1,128)S(1)}, u32[]{:S(2)}, u32[]{:S(2)}) %collective-permute-start.13) | collective-permute-done | bytes 2080 | tf_op jit(solution)/shard_map/ppermute | solution.py:31
  158.2 6.4 %shard_map.131 = (f32[512,512]{1,0:T(8,128)}, f32[512,512]{1,0:T(8,128)}, f32[512,512]{1,0:T(8,128)}) custom-call(s32[1]{0:T(128)} %bitcast.2.core, f32[512,640]{1,0:T(8,128)} %bitcast.69, f32[512,640]{1,0:T(8,128)} %collective-permute-done.12.theirs, f32[2,512,512]{2,1,0:T(8,128)} %diag.1, f32[512,512]{1,0:T(8,128)} %link.1), custom_call_target="tpu_custom_call" | custom-call | flops 4831838208 | bytes 9437184 | tf_op jit(solution)/shard_map/pallas_call | solution.py:194
  (88 shorter events, 18.4 us)
Async XLA Ops:
  7.2 1.5 copy-start.10
  7.2 68.9 %all-gather.2.cloned.1.call-start = ((), (), s32[]{:S(2)}) async-start(), calls=%async_computation.5 | async-start | bytes 4718592 | tf_op jit(solution)/shard_map/all_gather | solution.py:237
  9.0 2.7 %collective-permute-start = (f32[2,128,256]{2,1,0:T(8,128)S(1)}, f32[2,128,256]{2,1,0:T(8,128)S(1)}, u32[]{:S(2)}, u32[]{:S(2)}) collective-permute-start(f32[2,128,256]{2,1,0:T(8,128)S(1)} %fusion.4), channel_id=1, source_target_pairs={{0,1},{1,0},{2,3},{3,2},{4,5},{5,4},{6,7},{7,6},{8,9},{9,8},{10,11... | collective-permute-start | bytes 786440 | tf_op jit(solution)/shard_map/ppermute | solution.py:31
  11.7 23.0 %collective-permute-start.1 = (f32[512,4096]{1,0:T(8,128)}, f32[512,4096]{1,0:T(8,128)}, u32[]{:S(2)}, u32[]{:S(2)}) collective-permute-start(f32[512,4096]{1,0:T(8,128)} %refs_1_.3), channel_id=1, source_target_pairs={{0,1},{1,0},{2,3},{3,2},{4,5},{5,4},{6,7},{7,6},{8,9},{9,8},{10,11... | collective-permute-start | bytes 25165832 | tf_op jit(solution)/shard_map/ppermute | solution.py:31
  13.1 9.8 %collective-permute-start.5 = (f32[256,512]{1,0:T(8,128)S(1)}, f32[256,512]{1,0:T(8,128)S(1)}, u32[]{:S(2)}, u32[]{:S(2)}) collective-permute-start(f32[256,512]{1,0:T(8,128)S(1)} %pad_maximum_fusion.1), channel_id=1, source_target_pairs={{0,2},{1,9},{2,4},{3,11},{4,6},{5,13},{6,0},{7,15},{8,10},{9,17},{... | collective-permute-start | bytes 1572872 | tf_op jit(solution)/shard_map/ppermute | solution.py:42
  14.6 13.3 %collective-permute-start.2 = (f32[256,512]{1,0:T(8,128)S(1)}, f32[256,512]{1,0:T(8,128)S(1)}, u32[]{:S(2)}, u32[]{:S(2)}) collective-permute-start(f32[256,512]{1,0:T(8,128)S(1)} %pad_maximum_fusion.1), channel_id=1, source_target_pairs={{0,6},{1,25},{2,0},{3,27},{4,2},{5,29},{6,4},{7,31},{8,14},{9,1},{... | collective-permute-start | bytes 1572872 | tf_op jit(solution)/shard_map/ppermute | solution.py:42
  16.1 13.6 %collective-permute-start.3 = (f32[256,512]{1,0:T(8,128)S(1)}, f32[256,512]{1,0:T(8,128)S(1)}, u32[]{:S(2)}, u32[]{:S(2)}) collective-permute-start(f32[256,512]{1,0:T(8,128)S(1)} %pad_maximum_fusion.1), channel_id=1, source_target_pairs={{0,4},{1,17},{2,6},{3,19},{4,0},{5,21},{6,2},{7,23},{8,12},{9,25},... | collective-permute-start | bytes 1572872 | tf_op jit(solution)/shard_map/ppermute | solution.py:42
  23.0 19.7 %collective-permute-start.6 = (f32[512,512]{1,0:T(8,128)S(1)}, f32[512,512]{1,0:T(8,128)}, u32[]{:S(2)}, u32[]{:S(2)}) collective-permute-start(f32[512,512]{1,0:T(8,128)S(1)} %pad_maximum_fusion.refs_4_), channel_id=1, source_target_pairs={{0,8},{1,3},{2,10},{3,5},{4,12},{5,7},{6,14},{7,1},{8,16},{9,11},{... | collective-permute-start | bytes 3145736 | tf_op jit(solution)/shard_map/ppermute | solution.py:42
  24.4 20.2 %collective-permute-start.7 = (f32[512,512]{1,0:T(8,128)S(1)}, f32[512,512]{1,0:T(8,128)}, u32[]{:S(2)}, u32[]{:S(2)}) collective-permute-start(f32[512,512]{1,0:T(8,128)S(1)} %pad_maximum_fusion.refs_4_), channel_id=1, source_target_pairs={{0,24},{1,7},{2,26},{3,1},{4,28},{5,3},{6,30},{7,5},{8,0},{9,15},{... | collective-permute-start | bytes 3145736 | tf_op jit(solution)/shard_map/ppermute | solution.py:42
  29.7 23.8 %collective-permute-start.4 = (f32[512,512]{1,0:T(8,128)S(1)}, f32[512,512]{1,0:T(8,128)S(1)}, u32[]{:S(2)}, u32[]{:S(2)}) collective-permute-start(f32[512,512]{1,0:T(8,128)S(1)} %constant_dynamic-update-slice_fusion.refs_5_), channel_id=1, source_target_pairs={{0,24},{1,7},{2,26},{3,1},{4,28},{5,3},{6,30},{7,5},{8,0},{9,15},{... | collective-permute-start | bytes 3145736 | tf_op jit(solution)/shard_map/ppermute | solution.py:42
  34.7 8.5 %copy-start.11 = (f32[1,1,512]{2,1,0:T(1,128)S(1)}, f32[1,1,512]{2,1,0:T(1,128)}, u32[]{:S(2)}) copy-start(f32[1,1,512]{2,1,0:T(1,128)} %param.15) | copy-start | bytes 6148
  34.7 30.2 %collective-permute-start.9 = (f32[512,512]{1,0:T(8,128)S(1)}, f32[512,512]{1,0:T(8,128)}, u32[]{:S(2)}, u32[]{:S(2)}) collective-permute-start(f32[512,512]{1,0:T(8,128)S(1)} %constant_dynamic-update-slice_fusion.refs_5_), channel_id=1, source_target_pairs={{0,8},{1,3},{2,10},{3,5},{4,12},{5,7},{6,14},{7,1},{8,16},{9,11},{... | collective-permute-start | bytes 3145736 | tf_op jit(solution)/shard_map/ppermute | solution.py:42
  42.6 22.5 %collective-permute-start.10 = (f32[512,512]{1,0:T(8,128)}, f32[512,512]{1,0:T(8,128)}, u32[]{:S(2)}, u32[]{:S(2)}) collective-permute-start(f32[512,512]{1,0:T(8,128)} %collective-permute-done.6.refs_4_), channel_id=1, source_target_pairs={{0,8},{1,3},{2,10},{3,5},{4,12},{5,7},{6,14},{7,1},{8,16},{9,11},{... | collective-permute-start | bytes 3145736 | tf_op jit(solution)/shard_map/ppermute | solution.py:42
  53.5 22.5 %collective-permute-start.8 = (f32[512,512]{1,0:T(8,128)S(1)}, f32[512,512]{1,0:T(8,128)S(1)}, u32[]{:S(2)}, u32[]{:S(2)}) collective-permute-start(f32[512,512]{1,0:T(8,128)S(1)} %collective-permute-done.4.refs_5_), channel_id=1, source_target_pairs={{0,24},{1,7},{2,26},{3,1},{4,28},{5,3},{6,30},{7,5},{8,0},{9,15},{... | collective-permute-start | bytes 3145736 | tf_op jit(solution)/shard_map/ppermute | solution.py:42
  56.4 19.6 %all-to-all-start = ((f32[32,1,16]{2,1,0:T(1,128)}), f32[32,1,16]{2,1,0:T(1,128)S(1)}, u32[]{:S(2)}, u32[]{:S(2)}) async-start(f32[32,1,16]{2,1,0:T(1,128)} %bitcast.30), calls=%async_computation | async-start | bytes 32768 | tf_op jit(solution)/shard_map/all_to_all | solution.py:257
  64.6 54.4 %reduce-scatter.2.cloned.1.call-start = ((), (), s32[]{:S(2)}) async-start(), calls=%async_computation.6 | async-start | bytes 2621440 | tf_op jit(solution)/shard_map/reduce_scatter | solution.py:280
  110.6 10.3 %copy-start.12 = (s32[1,1,32]{2,1,0:T(1,128)S(1)}, s32[1,1,32]{2,1,0:T(1,128)}, u32[]{:S(2)}) copy-start(s32[1,1,32]{2,1,0:T(1,128)} %param.13) | copy-start | bytes 388
  110.6 10.3 %copy-start.13 = (s32[1,1,32]{2,1,0:T(1,128)S(1)}, s32[1,1,32]{2,1,0:T(1,128)}, u32[]{:S(2)}) copy-start(s32[1,1,32]{2,1,0:T(1,128)} %param.14) | copy-start | bytes 388
  111.4 10.0 %all-to-all-start.2 = ((f32[4,32,640]{2,1,0:T(8,128)}), f32[4,32,640]{2,1,0:T(8,128)S(1)}, u32[]{:S(2)}, u32[]{:S(2)}) async-start(f32[4,32,640]{2,1,0:T(8,128)} %broadcast_in_dim.4), calls=%async_computation.3 | async-start | bytes 655360 | tf_op jit(solution)/shard_map/all_to_all | solution.py:283
  119.1 3.0 %copy-start.5 = (f32[256,512]{1,0:T(8,128)S(1)}, f32[256,512]{1,0:T(8,128)}, u32[]{:S(2)}) copy-start(f32[256,512]{1,0:T(8,128)} %reduce-scatter.2.cloned.1.call-done) | copy-start | bytes 1572868
  120.2 1.9 %collective-permute-start.11 = (f32[128,512]{1,0:T(8,128)S(1)}, f32[128,512]{1,0:T(8,128)S(1)}, u32[]{:S(2)}, u32[]{:S(2)}) collective-permute-start(f32[128,512]{1,0:T(8,128)S(1)} %slice_select_fusion), channel_id=1, source_target_pairs={{0,1},{1,0},{2,3},{3,2},{4,5},{5,4},{6,7},{7,6},{8,9},{9,8},{10,11... | collective-permute-start | bytes 786440 | tf_op jit(solution)/shard_map/ppermute | solution.py:31
  152.7 5.5 %copy-start.6 = (f32[16,32,640]{2,1,0:T(8,128)}, f32[16,32,640]{2,1,0:T(8,128)S(1)}, u32[]{:S(2)}) copy-start(f32[16,32,640]{2,1,0:T(8,128)S(1)} %slice.100) | copy-start | bytes 3932164
  152.7 5.5 %collective-permute-start.12 = (f32[512,640]{1,0:T(8,128)S(1)}, f32[512,640]{1,0:T(8,128)}, u32[]{:S(2)}, u32[]{:S(2)}) collective-permute-start(f32[512,640]{1,0:T(8,128)S(1)} %bitcast.68), channel_id=1, source_target_pairs={{0,1},{1,0},{2,3},{3,2},{4,5},{5,4},{6,7},{7,6},{8,9},{9,8},{10,11... | collective-permute-start | bytes 3932168 | tf_op jit(solution)/shard_map/ppermute | solution.py:31
  155.1 2.5 %collective-permute-start.13 = (f32[1,512]{1,0:T(1,128)S(1)}, f32[1,512]{1,0:T(1,128)S(1)}, u32[]{:S(2)}, u32[]{:S(2)}) collective-permute-start(f32[1,512]{1,0:T(1,128)S(1)} %bitcast.73), channel_id=1, source_target_pairs={{0,1},{1,0},{2,3},{3,2},{4,5},{5,4},{6,7},{7,6},{8,9},{9,8},{10,11... | collective-permute-start | bytes 6152 | tf_op jit(solution)/shard_map/ppermute | solution.py:31
  (8 other events, 9.0 us)
Sparse Core Ops, SparseCore 0:
  13.1 34.4 all-gather.1
  87.1 31.9 reduce-scatter.1

commit v5 on v4

--- a/solution.py
+++ b/solution.py
@@ -199,6 +199,7 @@
         cost_estimate=pl.CostEstimate(
             flops=36 * 512 * 512 * 512, bytes_accessed=9 << 20, transcendentals=0
         ),
+        compiler_params=pltpu.CompilerParams(vmem_limit_bytes=40 << 20),
     )(core, mine, theirs, diag, link)
 
 

time: 172 us -> 169 us (0.983)
  Pallas kernels: 38.5 us -> 35.9 us
    pallas_call x1, Pallas kernels: 6.37 us -> 3.74 us  [close(): pl.pallas_call(close_kernel, in_specs=[pl.BlockSpec(memory_space=pltpu.SM...]
where the time goes in v5:
time: 169 us
  blocking collectives  52.3 us (31%)
  Pallas kernels  35.9 us (21%)
  starting transfers between devices  33.6 us (20%)
  waiting for transfers between devices  16.7 us (10%)
  between operations  14.4 us (9%)
  local copies, waits for them, and re-layouts  10.6 us (6%)
  other arithmetic  4.2 us (2%)
    pallas_call x4, Pallas kernels, add_product(): pl.pallas_call(functools.partial(product_kernel, len(pieces), has_total,...  32.1 us
    all_to_all x1, blocking collectives, local(): message = lax.all_to_all(message, plane, 0, 0, tiled=True)  28.7 us
    all_to_all x1, blocking collectives, local(): lax.all_to_all(part.reshape(16, 32, 640), plane, 0, 0, tiled=True).sum(0)  23.6 us
    ppermute x9, starting transfers between devices, hop(): return lax.ppermute(value, COL, pairs)  16 us
    ppermute x9, waiting for transfers between devices, hop(): return lax.ppermute(value, COL, pairs)  8.64 us
    unnamed x31, local copies, waits for them, and re-layouts  8.3 us
    all_to_all x1, starting transfers between devices, local(): weights = lax.all_to_all(weights, COL, 0, 0, tiled=True)  8.21 us
    ppermute x5, starting transfers between devices, swap_core(): return lax.ppermute(value, 'core', [(0, 1), (1, 0)])  5.02 us
  transfers between devices with their start and end apart: 18, of which 10 were waited for; matrix products, arithmetic and copies ran while one was open for 4% of the time, Pallas kernels for 14%

profile of v5, /device:TPU:1, one launch (start us, length us, event | category | flops | bytes accessed | tf_op | source)
XLA Modules:
  0.0 168.6 jit_solution(16034523464921972161)
XLA Ops:
  9.0 1.5 collective-permute-start
  13.1 1.4 collective-permute-start.5
  14.6 1.5 collective-permute-start.2
  16.1 1.6 collective-permute-start.3
  17.7 5.2 %collective-permute-done.5 = f32[256,512]{1,0:T(8,128)S(1)} collective-permute-done((f32[256,512]{1,0:T(8,128)S(1)}, f32[256,512]{1,0:T(8,128)S(1)}, u32[]{:S(2)}, u32[]{:S(2)}) %collective-permute-start.5) | collective-permute-done | bytes 524320 | tf_op jit(solution)/shard_map/ppermute | solution.py:42
  23.0 1.4 collective-permute-start.6
  24.4 2.5 %collective-permute-start.7 = (f32[512,512]{1,0:T(8,128)S(1)}, f32[512,512]{1,0:T(8,128)}, u32[]{:S(2)}, u32[]{:S(2)}) collective-permute-start(f32[512,512]{1,0:T(8,128)S(1)} %pad_maximum_fusion.refs_4_), channel_id=1, source_target_pairs={{0,24},{1,7},{2,26},{3,1},{4,28},{5,3},{6,30},{7,5},{8,0},{9,15},{... | collective-permute-start | bytes 3145736 | tf_op jit(solution)/shard_map/ppermute | solution.py:42
  27.9 1.8 %collective-permute-done.3 = f32[256,512]{1,0:T(8,128)S(1)} collective-permute-done((f32[256,512]{1,0:T(8,128)S(1)}, f32[256,512]{1,0:T(8,128)S(1)}, u32[]{:S(2)}, u32[]{:S(2)}) %collective-permute-start.3) | collective-permute-done | bytes 524320 | tf_op jit(solution)/shard_map/ppermute | solution.py:42
  29.7 4.9 %collective-permute-start.4 = (f32[512,512]{1,0:T(8,128)S(1)}, f32[512,512]{1,0:T(8,128)S(1)}, u32[]{:S(2)}, u32[]{:S(2)}) collective-permute-start(f32[512,512]{1,0:T(8,128)S(1)} %constant_dynamic-update-slice_fusion.refs_5_), channel_id=1, source_target_pairs={{0,24},{1,7},{2,26},{3,1},{4,28},{5,3},{6,30},{7,5},{8,0},{9,15},{... | collective-permute-start | bytes 3145736 | tf_op jit(solution)/shard_map/ppermute | solution.py:42
  34.7 6.2 %shard_map.127.refs_6_ = f32[1024,512]{1,0:T(8,128)S(1)} custom-call(s32[5]{0:T(128)S(1)} %stack.79.order, f32[512,4096]{1,0:T(8,128)} %refs_1_.3, f32[512,4096]{1,0:T(8,128)} %refs_1_.3, f32[512,4096]{1,0:T(8,128)} %collective-permute-done.1.refs_2_.refs_3_, f32[512,4096]{1,0:T(8,128)} %collective-permute-done.1.refs_2_.refs_3_, ...), custom_call_target="tpu_custom_call" | custom-call | flops 3221225472 | bytes 5242880 | tf_op jit(solution)/shard_map/pallas_call | solution.py:108
  40.9 1.3 copy-done
  44.6 7.6 %shard_map.128.refs_7_ = f32[1024,512]{1,0:T(8,128)S(1)} custom-call(s32[5]{0:T(128)S(1)} %stack.74.order, f32[512,4096]{1,0:T(8,128)} %refs_1_.3, f32[512,4096]{1,0:T(8,128)} %refs_1_.3, f32[512,4096]{1,0:T(8,128)} %collective-permute-done.1.refs_2_.refs_3_, f32[512,4096]{1,0:T(8,128)} %collective-permute-done.1.refs_2_.refs_3_, ...), custom_call_target="tpu_custom_call" | custom-call | flops 3221225472 | bytes 5242880 | tf_op jit(solution)/shard_map/pallas_call | solution.py:108
  53.5 2.7 %collective-permute-start.8 = (f32[512,512]{1,0:T(8,128)S(1)}, f32[512,512]{1,0:T(8,128)S(1)}, u32[]{:S(2)}, u32[]{:S(2)}) collective-permute-start(f32[512,512]{1,0:T(8,128)S(1)} %collective-permute-done.4.refs_5_), channel_id=1, source_target_pairs={{0,24},{1,7},{2,26},{3,1},{4,28},{5,3},{6,30},{7,5},{8,0},{9,15},{... | collective-permute-start | bytes 3145736 | tf_op jit(solution)/shard_map/ppermute | solution.py:42
  56.4 8.2 %all-to-all-start = ((f32[32,1,16]{2,1,0:T(1,128)}), f32[32,1,16]{2,1,0:T(1,128)S(1)}, u32[]{:S(2)}, u32[]{:S(2)}) async-start(f32[32,1,16]{2,1,0:T(1,128)} %bitcast.30), calls=%async_computation | async-start | bytes 32768 | tf_op jit(solution)/shard_map/all_to_all | solution.py:258
  65.1 9.6 %shard_map.129.refs_5_ = f32[1024,512]{1,0:T(8,128)S(1)} custom-call(s32[7]{0:T(128)S(1)} %stack.86.order, f32[512,4096]{1,0:T(8,128)} %refs_1_.3, f32[512,4096]{1,0:T(8,128)} %refs_1_.3, f32[512,4096]{1,0:T(8,128)} %collective-permute-done.1.refs_2_.refs_3_, f32[512,4096]{1,0:T(8,128)} %collective-permute-done.1.refs_2_.refs_3_, ...), custom_call_target="tpu_custom_call" | custom-call | flops 4831838208 | bytes 7864320 | tf_op jit(solution)/shard_map/pallas_call | solution.py:108
  74.7 1.3 copy-done.2
  78.2 8.7 %shard_map.130 = (f32[1024,512]{1,0:T(8,128)}, f32[512,640]{1,0:T(8,128)S(1)}) custom-call(s32[3]{0:T(128)S(1)} %pad_add_fusion.order, f32[512,4096]{1,0:T(8,128)} %refs_1_.3, f32[512,4096]{1,0:T(8,128)} %refs_1_.3, f32[512,4096]{1,0:T(8,128)} %collective-permute-done.1.refs_2_.refs_3_, f32[512,4096]{1,0:T(8,128)} %collective-permute-done.1.refs_2_.refs_3_, ...), custom_call_target="tpu_custom_call" | custom-call | flops 1610612736 | bytes 2621440 | tf_op jit(solution)/shard_map/pallas_call | solution.py:108
  87.0 23.6 %all_to_all.27 = f32[16,32,640]{2,1,0:T(8,128)S(1)} all-to-all(f32[16,32,640]{2,1,0:T(8,128)S(1)} %bitcast.68), channel_id=1, replica_groups=mesh['x'=4,'y'=4,'z'=4,'core'=2] {'y','z'}, dimensions={0} | all-to-all | bytes 2621440 | tf_op jit(solution)/shard_map/all_to_all | solution.py:282
  111.4 4.1 %all-to-all-start.2 = ((f32[4,32,640]{2,1,0:T(8,128)}), f32[4,32,640]{2,1,0:T(8,128)S(1)}, u32[]{:S(2)}, u32[]{:S(2)}) async-start(f32[4,32,640]{2,1,0:T(8,128)} %broadcast_in_dim.4), calls=%async_computation.3 | async-start | bytes 655360 | tf_op jit(solution)/shard_map/all_to_all | solution.py:284
  115.5 3.6 %reduce-scatter.2.cloned.1.call-done = f32[256,512]{1,0:T(8,128)} async-done(((f32[1024,512]{1,0:T(8,128)}), f32[256,512]{1,0:T(8,128)}) %reduce-scatter.2.cloned.1.call-update) | async-done | bytes 524304 | tf_op jit(solution)/shard_map/reduce_scatter | solution.py:281
  123.6 28.7 %all_to_all.28 = f32[16,32,768]{2,1,0:T(8,128)S(1)} all-to-all(f32[16,32,768]{2,1,0:T(8,128)S(1)} %select_maximum_fusion), channel_id=1, replica_groups=mesh['x'=4,'y'=4,'z'=4,'core'=2] {'y','z'}, dimensions={0} | all-to-all | bytes 3145728 | tf_op jit(solution)/shard_map/all_to_all | solution.py:295
  152.4 2.4 %collective-permute-start.12 = (f32[512,640]{1,0:T(8,128)S(1)}, f32[512,640]{1,0:T(8,128)S(1)}, u32[]{:S(2)}, u32[]{:S(2)}) collective-permute-start(f32[512,640]{1,0:T(8,128)S(1)} %bitcast.66), channel_id=1, source_target_pairs={{0,1},{1,0},{2,3},{3,2},{4,5},{5,4},{6,7},{7,6},{8,9},{9,8},{10,11... | collective-permute-start | bytes 3932168 | tf_op jit(solution)/shard_map/ppermute | solution.py:31
  154.9 2.5 %collective-permute-done.13 = f32[1,512]{1,0:T(1,128)S(1)} collective-permute-done((f32[1,512]{1,0:T(1,128)S(1)}, f32[1,512]{1,0:T(1,128)S(1)}, u32[]{:S(2)}, u32[]{:S(2)}) %collective-permute-start.13) | collective-permute-done | bytes 2080 | tf_op jit(solution)/shard_map/ppermute | solution.py:31
  158.0 3.7 %shard_map.131 = (f32[512,512]{1,0:T(8,128)}, f32[512,512]{1,0:T(8,128)}, f32[512,512]{1,0:T(8,128)}) custom-call(s32[1]{0:T(128)} %bitcast.2.core, f32[512,640]{1,0:T(8,128)S(1)} %bitcast.67, f32[512,640]{1,0:T(8,128)S(1)} %collective-permute-done.12.theirs, f32[2,512,512]{2,1,0:T(8,128)S(1)} %copy-done.6, f32[512,512]{1,0:T(8,128)S(1)} %copy-done.5), custom_call_target="tpu_custom_call" | custom-call | flops 4831838208 | bytes 9437184 | tf_op jit(solution)/shard_map/pallas_call | solution.py:194
  (88 shorter events, 18.2 us)
Async XLA Ops:
  7.2 1.5 copy-start.10
  7.2 68.9 %all-gather.2.cloned.1.call-start = ((), (), s32[]{:S(2)}) async-start(), calls=%async_computation.5 | async-start | bytes 4718592 | tf_op jit(solution)/shard_map/all_gather | solution.py:238
  9.0 2.7 %collective-permute-start = (f32[2,128,256]{2,1,0:T(8,128)S(1)}, f32[2,128,256]{2,1,0:T(8,128)S(1)}, u32[]{:S(2)}, u32[]{:S(2)}) collective-permute-start(f32[2,128,256]{2,1,0:T(8,128)S(1)} %fusion.4), channel_id=1, source_target_pairs={{0,1},{1,0},{2,3},{3,2},{4,5},{5,4},{6,7},{7,6},{8,9},{9,8},{10,11... | collective-permute-start | bytes 786440 | tf_op jit(solution)/shard_map/ppermute | solution.py:31
  11.7 23.0 %collective-permute-start.1 = (f32[512,4096]{1,0:T(8,128)}, f32[512,4096]{1,0:T(8,128)}, u32[]{:S(2)}, u32[]{:S(2)}) collective-permute-start(f32[512,4096]{1,0:T(8,128)} %refs_1_.3), channel_id=1, source_target_pairs={{0,1},{1,0},{2,3},{3,2},{4,5},{5,4},{6,7},{7,6},{8,9},{9,8},{10,11... | collective-permute-start | bytes 25165832 | tf_op jit(solution)/shard_map/ppermute | solution.py:31
  13.1 9.8 %collective-permute-start.5 = (f32[256,512]{1,0:T(8,128)S(1)}, f32[256,512]{1,0:T(8,128)S(1)}, u32[]{:S(2)}, u32[]{:S(2)}) collective-permute-start(f32[256,512]{1,0:T(8,128)S(1)} %pad_maximum_fusion.1), channel_id=1, source_target_pairs={{0,2},{1,9},{2,4},{3,11},{4,6},{5,13},{6,0},{7,15},{8,10},{9,17},{... | collective-permute-start | bytes 1572872 | tf_op jit(solution)/shard_map/ppermute | solution.py:42
  14.6 13.3 %collective-permute-start.2 = (f32[256,512]{1,0:T(8,128)S(1)}, f32[256,512]{1,0:T(8,128)S(1)}, u32[]{:S(2)}, u32[]{:S(2)}) collective-permute-start(f32[256,512]{1,0:T(8,128)S(1)} %pad_maximum_fusion.1), channel_id=1, source_target_pairs={{0,6},{1,25},{2,0},{3,27},{4,2},{5,29},{6,4},{7,31},{8,14},{9,1},{... | collective-permute-start | bytes 1572872 | tf_op jit(solution)/shard_map/ppermute | solution.py:42
  16.1 13.6 %collective-permute-start.3 = (f32[256,512]{1,0:T(8,128)S(1)}, f32[256,512]{1,0:T(8,128)S(1)}, u32[]{:S(2)}, u32[]{:S(2)}) collective-permute-start(f32[256,512]{1,0:T(8,128)S(1)} %pad_maximum_fusion.1), channel_id=1, source_target_pairs={{0,4},{1,17},{2,6},{3,19},{4,0},{5,21},{6,2},{7,23},{8,12},{9,25},... | collective-permute-start | bytes 1572872 | tf_op jit(solution)/shard_map/ppermute | solution.py:42
  23.0 19.7 %collective-permute-start.6 = (f32[512,512]{1,0:T(8,128)S(1)}, f32[512,512]{1,0:T(8,128)}, u32[]{:S(2)}, u32[]{:S(2)}) collective-permute-start(f32[512,512]{1,0:T(8,128)S(1)} %pad_maximum_fusion.refs_4_), channel_id=1, source_target_pairs={{0,8},{1,3},{2,10},{3,5},{4,12},{5,7},{6,14},{7,1},{8,16},{9,11},{... | collective-permute-start | bytes 3145736 | tf_op jit(solution)/shard_map/ppermute | solution.py:42
  24.4 20.2 %collective-permute-start.7 = (f32[512,512]{1,0:T(8,128)S(1)}, f32[512,512]{1,0:T(8,128)}, u32[]{:S(2)}, u32[]{:S(2)}) collective-permute-start(f32[512,512]{1,0:T(8,128)S(1)} %pad_maximum_fusion.refs_4_), channel_id=1, source_target_pairs={{0,24},{1,7},{2,26},{3,1},{4,28},{5,3},{6,30},{7,5},{8,0},{9,15},{... | collective-permute-start | bytes 3145736 | tf_op jit(solution)/shard_map/ppermute | solution.py:42
  29.7 23.8 %collective-permute-start.4 = (f32[512,512]{1,0:T(8,128)S(1)}, f32[512,512]{1,0:T(8,128)S(1)}, u32[]{:S(2)}, u32[]{:S(2)}) collective-permute-start(f32[512,512]{1,0:T(8,128)S(1)} %constant_dynamic-update-slice_fusion.refs_5_), channel_id=1, source_target_pairs={{0,24},{1,7},{2,26},{3,1},{4,28},{5,3},{6,30},{7,5},{8,0},{9,15},{... | collective-permute-start | bytes 3145736 | tf_op jit(solution)/shard_map/ppermute | solution.py:42
  34.7 8.5 %copy-start.11 = (f32[1,1,512]{2,1,0:T(1,128)S(1)}, f32[1,1,512]{2,1,0:T(1,128)}, u32[]{:S(2)}) copy-start(f32[1,1,512]{2,1,0:T(1,128)} %param.15) | copy-start | bytes 6148
  34.7 30.2 %collective-permute-start.9 = (f32[512,512]{1,0:T(8,128)S(1)}, f32[512,512]{1,0:T(8,128)}, u32[]{:S(2)}, u32[]{:S(2)}) collective-permute-start(f32[512,512]{1,0:T(8,128)S(1)} %constant_dynamic-update-slice_fusion.refs_5_), channel_id=1, source_target_pairs={{0,8},{1,3},{2,10},{3,5},{4,12},{5,7},{6,14},{7,1},{8,16},{9,11},{... | collective-permute-start | bytes 3145736 | tf_op jit(solution)/shard_map/ppermute | solution.py:42
  42.6 22.5 %collective-permute-start.10 = (f32[512,512]{1,0:T(8,128)}, f32[512,512]{1,0:T(8,128)}, u32[]{:S(2)}, u32[]{:S(2)}) collective-permute-start(f32[512,512]{1,0:T(8,128)} %collective-permute-done.6.refs_4_), channel_id=1, source_target_pairs={{0,8},{1,3},{2,10},{3,5},{4,12},{5,7},{6,14},{7,1},{8,16},{9,11},{... | collective-permute-start | bytes 3145736 | tf_op jit(solution)/shard_map/ppermute | solution.py:42
  53.5 22.5 %collective-permute-start.8 = (f32[512,512]{1,0:T(8,128)S(1)}, f32[512,512]{1,0:T(8,128)S(1)}, u32[]{:S(2)}, u32[]{:S(2)}) collective-permute-start(f32[512,512]{1,0:T(8,128)S(1)} %collective-permute-done.4.refs_5_), channel_id=1, source_target_pairs={{0,24},{1,7},{2,26},{3,1},{4,28},{5,3},{6,30},{7,5},{8,0},{9,15},{... | collective-permute-start | bytes 3145736 | tf_op jit(solution)/shard_map/ppermute | solution.py:42
  56.4 19.6 %all-to-all-start = ((f32[32,1,16]{2,1,0:T(1,128)}), f32[32,1,16]{2,1,0:T(1,128)S(1)}, u32[]{:S(2)}, u32[]{:S(2)}) async-start(f32[32,1,16]{2,1,0:T(1,128)} %bitcast.30), calls=%async_computation | async-start | bytes 32768 | tf_op jit(solution)/shard_map/all_to_all | solution.py:258
  64.6 54.4 %reduce-scatter.2.cloned.1.call-start = ((), (), s32[]{:S(2)}) async-start(), calls=%async_computation.6 | async-start | bytes 2621440 | tf_op jit(solution)/shard_map/reduce_scatter | solution.py:281
  110.6 10.3 %copy-start.12 = (s32[1,1,32]{2,1,0:T(1,128)S(1)}, s32[1,1,32]{2,1,0:T(1,128)}, u32[]{:S(2)}) copy-start(s32[1,1,32]{2,1,0:T(1,128)} %param.13) | copy-start | bytes 388
  110.6 10.3 %copy-start.13 = (s32[1,1,32]{2,1,0:T(1,128)S(1)}, s32[1,1,32]{2,1,0:T(1,128)}, u32[]{:S(2)}) copy-start(s32[1,1,32]{2,1,0:T(1,128)} %param.14) | copy-start | bytes 388
  111.4 10.0 %all-to-all-start.2 = ((f32[4,32,640]{2,1,0:T(8,128)}), f32[4,32,640]{2,1,0:T(8,128)S(1)}, u32[]{:S(2)}, u32[]{:S(2)}) async-start(f32[4,32,640]{2,1,0:T(8,128)} %broadcast_in_dim.4), calls=%async_computation.3 | async-start | bytes 655360 | tf_op jit(solution)/shard_map/all_to_all | solution.py:284
  119.1 3.0 %copy-start.7 = (f32[256,512]{1,0:T(8,128)S(1)}, f32[256,512]{1,0:T(8,128)}, u32[]{:S(2)}) copy-start(f32[256,512]{1,0:T(8,128)} %reduce-scatter.2.cloned.1.call-done) | copy-start | bytes 1572868
  120.2 1.9 %collective-permute-start.11 = (f32[128,512]{1,0:T(8,128)S(1)}, f32[128,512]{1,0:T(8,128)S(1)}, u32[]{:S(2)}, u32[]{:S(2)}) collective-permute-start(f32[128,512]{1,0:T(8,128)S(1)} %slice_select_fusion), channel_id=1, source_target_pairs={{0,1},{1,0},{2,3},{3,2},{4,5},{5,4},{6,7},{7,6},{8,9},{9,8},{10,11... | collective-permute-start | bytes 786440 | tf_op jit(solution)/shard_map/ppermute | solution.py:31
  152.3 5.7 %copy-start.6 = (f32[2,512,512]{2,1,0:T(8,128)S(1)}, f32[2,512,512]{2,1,0:T(8,128)}, u32[]{:S(2)}) copy-start(f32[2,512,512]{2,1,0:T(8,128)} %diag.1) | copy-start | bytes 6291460
  152.4 5.6 %collective-permute-start.12 = (f32[512,640]{1,0:T(8,128)S(1)}, f32[512,640]{1,0:T(8,128)S(1)}, u32[]{:S(2)}, u32[]{:S(2)}) collective-permute-start(f32[512,640]{1,0:T(8,128)S(1)} %bitcast.66), channel_id=1, source_target_pairs={{0,1},{1,0},{2,3},{3,2},{4,5},{5,4},{6,7},{7,6},{8,9},{9,8},{10,11... | collective-permute-start | bytes 3932168 | tf_op jit(solution)/shard_map/ppermute | solution.py:31
  154.8 2.6 %collective-permute-start.13 = (f32[1,512]{1,0:T(1,128)S(1)}, f32[1,512]{1,0:T(1,128)S(1)}, u32[]{:S(2)}, u32[]{:S(2)}) collective-permute-start(f32[1,512]{1,0:T(1,128)S(1)} %bitcast.73), channel_id=1, source_target_pairs={{0,1},{1,0},{2,3},{3,2},{4,5},{5,4},{6,7},{7,6},{8,9},{9,8},{10,11... | collective-permute-start | bytes 6152 | tf_op jit(solution)/shard_map/ppermute | solution.py:31
  (8 other events, 9.1 us)
Sparse Core Ops, SparseCore 0:
  13.1 34.4 all-gather.1
  87.1 31.9 reduce-scatter.1
